TPU v7x, 32 devices: a whole 2x2x4 slice. The times are simulated.
32 devices in a mesh: dp: 2 (over x), seq: 8 (over z, core), tensor: 2 (over y).
Axes of the slice: x: 2, y: 2, z: 4, core: 2. Of those that a mesh axis runs over, the one named last changes fastest.
Arguments:
- tokens: bfloat16 [2, 4096, 768], P('dp', 'seq'), may hold values from -6 to 6
- doc_ids: int32 [2, 4096], P('dp'), may hold values from 0 to 15, as said below
- memory: bfloat16 [20, 768], replicated, may hold values from -6 to 6
- qkv_weight: bfloat16 [768, 3, 768], P(None, None, 'tensor'), may hold values from -0.21875 to 0.21875
- query_bias: float32 [768], P('tensor'), may hold values from -3 to 3
- value_bias: float32 [768], P('tensor'), may hold values from -3 to 3
- out_weight: bfloat16 [768, 768], P(None, 'tensor'), may hold values from -1.75 to 1.75
- out_bias: float32 [768], replicated, may hold values from -1.75 to 1.75
- norm1_gain: float32 [768], replicated, may hold values from 0.5 to 1.5
- norm1_bias: float32 [768], replicated, may hold values from -1.75 to 1.75
- up_weight: bfloat16 [768, 3072], P(None, 'tensor'), may hold values from -0.21875 to 0.21875
- up_bias: float32 [3072], P('tensor'), may hold values from -3 to 3
- down_weight: bfloat16 [768, 3072], P(None, 'tensor'), may hold values from -0.109375 to 0.109375
- down_bias: float32 [768], replicated, may hold values from -1.75 to 1.75
- norm2_gain: float32 [768], replicated, may hold values from 0.5 to 1.5
- norm2_bias: float32 [768], replicated, may hold values from -1.75 to 1.75
- out_grad: bfloat16 [2, 4096, 768], P('dp', 'seq'), may hold values from -6 to 6
Outputs:
- output: bfloat16 [2, 4096, 768], P('dp', 'seq')
- input_grad: bfloat16 [2, 4096, 768], P('dp', 'seq')
- memory_grad: float32 [20, 768], replicated
- qkv_weight_grad: float32 [768, 3, 768], P('seq', None, 'tensor')
- query_bias_grad: float32 [768], P('tensor')
- value_bias_grad: float32 [768], P('tensor')
- out_weight_grad: float32 [768, 768], P('seq', 'tensor')
- out_bias_grad: float32 [768], P('seq')
- norm1_gain_grad: float32 [768], P('seq')
- norm1_bias_grad: float32 [768], P('seq')
- up_weight_grad: float32 [768, 3072], P('seq', 'tensor')
- up_bias_grad: float32 [3072], P('tensor')
- down_weight_grad: float32 [768, 3072], P('seq', 'tensor')
- down_bias_grad: float32 [768], P('seq')
- norm2_gain_grad: float32 [768], P('seq')
- norm2_bias_grad: float32 [768], P('seq')
Inputs may be any that keep to these rules, and one draw needn't show every extreme that they name: In every sequence doc_ids never fall, each document covers 21 to 1536 consecutive rows, every number of 0 to 15 is used, and one document has exactly 1536 rows.
All inputs are finite; a program needn't handle non-finite values.
Results may differ from a plain program's by a relative error of at most 0.024.
Values may be sent and summed in bfloat16 or wider, within the bound.
A program may use at most 192 MiB of HBM per device.

v0:
```python
import jax
import jax.numpy as jnp
from jax import lax
from jax.sharding import PartitionSpec as P

HEAD_DIM = 64
READ_ROWS = 10
REACH = 3


norm_eps = 1e-05


def shifted(value, axis, steps):
    count = lax.axis_size(axis)
    leading, last = (max(0, -steps), min(count, count - steps))
    return lax.ppermute(value, axis, [(source, source + steps) for source in range(leading, last)])


def memory_slots(id_row):
    count = id_row.shape[0]
    places = jnp.arange(count, dtype=jnp.int32)
    before = jnp.concatenate([jnp.full((1,), -1, jnp.int32), id_row[:-1]])
    after = jnp.concatenate([id_row[1:], jnp.full((1,), -1, jnp.int32)])
    starts = lax.cummax(jnp.where(id_row != before, places, 0), axis=0)
    finish = lax.cummin(jnp.where(id_row != after, places, count), axis=0, reverse=True)
    offset = places - starts
    behind = finish - places
    return jnp.where(
        offset < READ_ROWS, offset, jnp.where(behind < READ_ROWS, 2 * READ_ROWS - 1 - behind, -1)
    )


def normalize(hidden, gain, shift):
    centre = jnp.mean(hidden, axis=-1, keepdims=True)
    centred = hidden - centre
    spread = jnp.mean(centred * centred, axis=-1, keepdims=True)
    return centred * lax.rsqrt(spread + norm_eps) * gain + shift


def gelu_exact(values):
    return jax.nn.gelu(values, approximate=False)


def column_sums(matrix):
    return jnp.sum(matrix.astype(jnp.float32), axis=0)


def on_device(
    tokens,
    doc_ids,
    memory,
    qkv_weight,
    query_bias,
    value_bias,
    out_weight,
    out_bias,
    norm1_gain,
    norm1_bias,
    up_weight,
    up_bias,
    down_weight,
    down_bias,
    norm2_gain,
    norm2_bias,
    out_grad,
):
    row_count = tokens.shape[1]
    local_width = qkv_weight.shape[2]
    heads_here = local_width // HEAD_DIM
    reach_stretches = REACH
    piece_count = 2 * reach_stretches + 1
    scale_factor = HEAD_DIM ** (-0.5)
    block_rows = min(512, row_count)
    block_count = row_count // block_rows
    stretch_index = lax.axis_index("seq")
    id_row = doc_ids[0]
    own_ids = lax.dynamic_slice_in_dim(id_row, stretch_index * row_count, row_count, 0)
    all_slots = memory_slots(id_row)
    own_slots = lax.dynamic_slice_in_dim(all_slots, stretch_index * row_count, row_count, 0)
    is_memory = (own_slots >= 0)[:, None]
    selector = own_slots[:, None] == jnp.arange(2 * READ_ROWS, dtype=jnp.int32)[None, :]
    memory_rows = jnp.dot(
        selector.astype(jnp.bfloat16), memory, preferred_element_type=jnp.float32
    ).astype(jnp.bfloat16)
    source = jnp.where(is_memory, memory_rows, tokens[0])
    id_edge = jnp.full((reach_stretches * row_count,), -1, jnp.int32)
    padded_ids = jnp.concatenate([id_edge, id_row, id_edge])
    window_ids = lax.dynamic_slice_in_dim(
        padded_ids, stretch_index * row_count, piece_count * row_count, 0
    ).reshape(piece_count, row_count)
    projected = jnp.einsum("td,dcf->tcf", source, qkv_weight, preferred_element_type=jnp.float32)
    query_rows = (projected[:, 0] + query_bias).astype(jnp.bfloat16)
    key_rows = projected[:, 1].astype(jnp.bfloat16)
    value_rows = (projected[:, 2] + value_bias).astype(jnp.bfloat16)
    key_value = jnp.stack([key_rows, value_rows])
    window_list = []
    for offset in range(-reach_stretches, reach_stretches + 1):
        if offset == 0:
            window_list.append(key_value)
        else:
            window_list.append(shifted(key_value, "seq", -offset))
    window = jnp.stack(window_list)

    def score_piece(query_block, query_ids, piece_index):
        key_piece = window[piece_index, 0].reshape(row_count, heads_here, HEAD_DIM)
        raw_scores = (
            jnp.einsum("qhd,khd->hqk", query_block, key_piece, preferred_element_type=jnp.float32)
            * scale_factor
        )
        same_doc = (query_ids[:, None] == window_ids[piece_index][None, :])[None]
        return (raw_scores, same_doc)

    def forward_block(block_item):
        query_block, query_ids = block_item
        row_max = jnp.full((heads_here, block_rows), -1e30, jnp.float32)
        row_total = jnp.zeros((heads_here, block_rows), jnp.float32)
        for piece_index in range(piece_count):
            raw_scores, same_doc = score_piece(query_block, query_ids, piece_index)
            masked = jnp.where(same_doc, raw_scores, -1e30)
            new_max = jnp.maximum(row_max, jnp.max(masked, axis=-1))
            fresh = jnp.sum(jnp.where(same_doc, jnp.exp(masked - new_max[..., None]), 0.0), axis=-1)
            row_total = row_total * jnp.exp(row_max - new_max) + fresh
            row_max = new_max
        logsum = row_max + jnp.log(row_total)
        mixed_block = jnp.zeros((block_rows, heads_here, HEAD_DIM), jnp.float32)
        for piece_index in range(piece_count):
            raw_scores, same_doc = score_piece(query_block, query_ids, piece_index)
            weights = jnp.where(same_doc, jnp.exp(raw_scores - logsum[..., None]), 0.0).astype(
                jnp.bfloat16
            )
            value_piece = window[piece_index, 1].reshape(row_count, heads_here, HEAD_DIM)
            mixed_block = mixed_block + jnp.einsum(
                "hqk,khd->qhd", weights, value_piece, preferred_element_type=jnp.float32
            )
        return (mixed_block, logsum)

    query_blocks = query_rows.reshape(block_count, block_rows, heads_here, HEAD_DIM)
    id_blocks = own_ids.reshape(block_count, block_rows)
    mixed_parts, logsums = lax.map(forward_block, (query_blocks, id_blocks))
    mixed_full = mixed_parts.reshape(row_count, local_width)
    mixed_low = mixed_full.astype(jnp.bfloat16)
    attn_part = jnp.einsum("tf,of->to", mixed_low, out_weight, preferred_element_type=jnp.float32)
    branch = lax.psum(attn_part.astype(jnp.bfloat16), "tensor").astype(jnp.float32) + out_bias
    first_input = source.astype(jnp.float32) + branch
    first_out, first_pull = jax.vjp(normalize, first_input, norm1_gain, norm1_bias)
    first_low = first_out.astype(jnp.bfloat16)
    up_proj = jnp.dot(first_low, up_weight, preferred_element_type=jnp.float32) + up_bias
    act_full, gelu_pull = jax.vjp(gelu_exact, up_proj)
    act_low = act_full.astype(jnp.bfloat16)
    down_part = jnp.einsum("tf,of->to", act_low, down_weight, preferred_element_type=jnp.float32)
    down_out = lax.psum(down_part.astype(jnp.bfloat16), "tensor").astype(jnp.float32) + down_bias
    second_input = first_out + down_out
    result, second_pull = jax.vjp(normalize, second_input, norm2_gain, norm2_bias)
    output = result.astype(jnp.bfloat16)[None]
    grad_second, grad_gain2, grad_shift2 = second_pull(out_grad[0].astype(jnp.float32))
    down_grad = grad_second.astype(jnp.bfloat16)
    grad_down_bias = column_sums(down_grad)
    grad_down_weight = jnp.einsum(
        "to,tf->of", down_grad, act_low, preferred_element_type=jnp.float32
    )
    act_grad = jnp.einsum("to,of->tf", down_grad, down_weight, preferred_element_type=jnp.float32)
    up_grad = gelu_pull(act_grad)[0].astype(jnp.bfloat16)
    grad_up_bias = column_sums(up_grad)
    grad_up_weight = jnp.einsum("td,tf->df", first_low, up_grad, preferred_element_type=jnp.float32)
    hidden_part = jnp.einsum("tf,df->td", up_grad, up_weight, preferred_element_type=jnp.float32)
    grad_first = grad_second + lax.psum(hidden_part.astype(jnp.bfloat16), "tensor").astype(
        jnp.float32
    )
    grad_input1, grad_gain1, grad_shift1 = first_pull(grad_first)
    branch_grad = grad_input1.astype(jnp.bfloat16)
    grad_out_bias = column_sums(branch_grad)
    grad_out_weight = jnp.einsum(
        "to,tf->of", branch_grad, mixed_low, preferred_element_type=jnp.float32
    )
    mixed_grad = jnp.einsum(
        "to,of->tf", branch_grad, out_weight, preferred_element_type=jnp.float32
    ).astype(jnp.bfloat16)
    along = jnp.sum(
        (mixed_grad.astype(jnp.float32) * mixed_full).reshape(row_count, heads_here, HEAD_DIM),
        axis=-1,
    )

    def backward_block(carried, block_item):
        query_block, query_ids, grad_block, logsum, along_block = block_item
        row_term = along_block.T[..., None]
        query_grad = jnp.zeros((block_rows, heads_here, HEAD_DIM), jnp.float32)
        updates = []
        for piece_index in range(piece_count):
            raw_scores, same_doc = score_piece(query_block, query_ids, piece_index)
            probs = jnp.where(same_doc, jnp.exp(raw_scores - logsum[..., None]), 0.0)
            key_piece = window[piece_index, 0].reshape(row_count, heads_here, HEAD_DIM)
            value_piece = window[piece_index, 1].reshape(row_count, heads_here, HEAD_DIM)
            value_grad = jnp.einsum(
                "hqk,qhd->khd",
                probs.astype(jnp.bfloat16),
                grad_block,
                preferred_element_type=jnp.float32,
            )
            prob_grad = jnp.einsum(
                "qhd,khd->hqk", grad_block, value_piece, preferred_element_type=jnp.float32
            )
            score_grad = (probs * (prob_grad - row_term)).astype(jnp.bfloat16)
            query_grad = query_grad + scale_factor * jnp.einsum(
                "hqk,khd->qhd", score_grad, key_piece, preferred_element_type=jnp.float32
            )
            key_grad = scale_factor * jnp.einsum(
                "hqk,qhd->khd", score_grad, query_block, preferred_element_type=jnp.float32
            )
            updates.append(jnp.stack([key_grad, value_grad]))
        return (carried + jnp.stack(updates), query_grad)

    start_grads = jnp.zeros((piece_count, 2, row_count, heads_here, HEAD_DIM), jnp.float32)
    grad_blocks = mixed_grad.reshape(block_count, block_rows, heads_here, HEAD_DIM)
    along_blocks = along.reshape(block_count, block_rows, heads_here)
    window_grads, query_grads = lax.scan(
        backward_block, start_grads, (query_blocks, id_blocks, grad_blocks, logsums, along_blocks)
    )
    window_grads = window_grads.reshape(piece_count, 2, row_count, local_width)
    owned = window_grads[reach_stretches]
    for offset in range(-reach_stretches, reach_stretches + 1):
        if offset != 0:
            owned = owned + shifted(
                window_grads[offset + reach_stretches].astype(jnp.bfloat16), "seq", offset
            ).astype(jnp.float32)
    query_total = query_grads.reshape(row_count, local_width)
    proj_grad = jnp.stack([query_total, owned[0], owned[1]], axis=1).astype(jnp.bfloat16)
    grad_query_bias = column_sums(proj_grad[:, 0])
    grad_value_bias = column_sums(proj_grad[:, 2])
    grad_qkv_weight = jnp.einsum(
        "td,tcf->dcf", source, proj_grad, preferred_element_type=jnp.float32
    )
    input_part = jnp.einsum(
        "tcf,dcf->td", proj_grad, qkv_weight, preferred_element_type=jnp.float32
    )
    input_total = grad_input1 + lax.psum(input_part.astype(jnp.bfloat16), "tensor").astype(
        jnp.float32
    )
    grad_memory = jnp.dot(
        selector.astype(jnp.float32).T, input_total, precision=lax.Precision.HIGHEST
    )
    input_grad = jnp.where(is_memory, 0.0, input_total).astype(jnp.bfloat16)[None]
    reduced = (
        lax.psum_scatter(
            grad_qkv_weight.astype(jnp.bfloat16), "seq", scatter_dimension=0, tiled=True
        ).astype(jnp.float32),
        lax.psum_scatter(
            grad_out_weight.astype(jnp.bfloat16), "seq", scatter_dimension=0, tiled=True
        ).astype(jnp.float32),
        lax.psum_scatter(
            grad_out_bias.astype(jnp.bfloat16), "seq", scatter_dimension=0, tiled=True
        ).astype(jnp.float32),
        lax.psum_scatter(
            grad_gain1.astype(jnp.bfloat16), "seq", scatter_dimension=0, tiled=True
        ).astype(jnp.float32),
        lax.psum_scatter(
            grad_shift1.astype(jnp.bfloat16), "seq", scatter_dimension=0, tiled=True
        ).astype(jnp.float32),
        lax.psum_scatter(
            grad_up_weight.astype(jnp.bfloat16), "seq", scatter_dimension=0, tiled=True
        ).astype(jnp.float32),
        lax.psum_scatter(
            grad_down_weight.astype(jnp.bfloat16), "seq", scatter_dimension=0, tiled=True
        ).astype(jnp.float32),
        lax.psum_scatter(
            grad_down_bias.astype(jnp.bfloat16), "seq", scatter_dimension=0, tiled=True
        ).astype(jnp.float32),
        lax.psum_scatter(
            grad_gain2.astype(jnp.bfloat16), "seq", scatter_dimension=0, tiled=True
        ).astype(jnp.float32),
        lax.psum_scatter(
            grad_shift2.astype(jnp.bfloat16), "seq", scatter_dimension=0, tiled=True
        ).astype(jnp.float32),
    )
    reduced = (
        lax.psum(reduced[0].astype(jnp.bfloat16), "dp").astype(jnp.float32),
        lax.psum(reduced[1].astype(jnp.bfloat16), "dp").astype(jnp.float32),
        lax.psum(reduced[2].astype(jnp.bfloat16), "dp").astype(jnp.float32),
        lax.psum(reduced[3].astype(jnp.bfloat16), "dp").astype(jnp.float32),
        lax.psum(reduced[4].astype(jnp.bfloat16), "dp").astype(jnp.float32),
        lax.psum(reduced[5].astype(jnp.bfloat16), "dp").astype(jnp.float32),
        lax.psum(reduced[6].astype(jnp.bfloat16), "dp").astype(jnp.float32),
        lax.psum(reduced[7].astype(jnp.bfloat16), "dp").astype(jnp.float32),
        lax.psum(reduced[8].astype(jnp.bfloat16), "dp").astype(jnp.float32),
        lax.psum(reduced[9].astype(jnp.bfloat16), "dp").astype(jnp.float32),
    )
    bias_sums = lax.psum(
        (grad_query_bias, grad_value_bias, grad_up_bias, grad_memory), ("dp", "seq")
    )
    return (
        output,
        input_grad,
        bias_sums[3],
        reduced[0],
        bias_sums[0],
        bias_sums[1],
        reduced[1],
        reduced[2],
        reduced[3],
        reduced[4],
        reduced[5],
        bias_sums[2],
        reduced[6],
        reduced[7],
        reduced[8],
        reduced[9],
    )


def solution(mesh):
    in_specs = (
        P("dp", "seq", None),
        P("dp", None),
        P(),
        P(None, None, "tensor"),
        P("tensor"),
        P("tensor"),
        P(None, "tensor"),
        P(),
        P(),
        P(),
        P(None, "tensor"),
        P("tensor"),
        P(None, "tensor"),
        P(),
        P(),
        P(),
        P("dp", "seq", None),
    )
    out_specs = (
        P("dp", "seq", None),
        P("dp", "seq", None),
        P(),
        P("seq", None, "tensor"),
        P("tensor"),
        P("tensor"),
        P("seq", "tensor"),
        P("seq"),
        P("seq"),
        P("seq"),
        P("seq", "tensor"),
        P("tensor"),
        P("seq", "tensor"),
        P("seq"),
        P("seq"),
        P("seq"),
    )
    return jax.shard_map(
        on_device, mesh=mesh, in_specs=in_specs, out_specs=out_specs, check_vma=False
    )
```

profile of v0, /device:TPU:0, one launch (start us, length us, event | category | flops | bytes accessed | tf_op | source)
XLA Modules:
  0.0 665.6 jit_solution(9818831797957123007)
XLA Ops:
  9.0 2.3 reduce-window.24
  14.0 2.6 fusion.49
  21.9 4.0 collective-permute-start.2
  25.9 5.5 collective-permute-start.1
  38.5 4.9 collective-permute-done.5
  47.4 3.9 collective-permute-done.4
  59.4 6.2 collective-permute-done
  66.5 3.8 select_reduce_fusion.7
  70.3 3.9 select_reduce_fusion.8
  80.8 7.6 %select_reduce_fusion = f32[6,512]{1,0:T(8,128)} fusion(f32[6,512,512]{1,2,0:T(8,128)} %get-tuple-element.189, f32[6,512]{1,0:T(8,128)S(1)} %get-tuple-element.142, pred[512,512]{0,1:T(8,128)(4,1)} %copy-done.58), kind=kLoop, calls=%fused_computation.14 | loop fusion | flops 7861248 | bytes 6578176 | tf_op jit(solution)/shard_map/while/body/eval_jaxpr/reduce_sum | solution.py:122
  88.3 4.9 select_reduce_fusion.1
  93.3 3.5 select_reduce_fusion.2
  96.7 3.1 select_reduce_fusion.3
  99.8 3.1 select_reduce_fusion.4
  102.9 3.1 select_reduce_fusion.5
  109.0 4.3 fusion.72
  113.4 4.2 fusion.75
  128.6 51.5 %all-reduce.17.cloned.1.call-done = bf16[512,768]{1,0:T(8,128)(2,1)} async-done(((bf16[512,768]{1,0:T(8,128)(2,1)}), bf16[512,768]{1,0:T(8,128)(2,1)}) %all-reduce.17.cloned.1.call-update) | async-done | bytes 786448 | tf_op jit(solution)/shard_map/psum | solution.py:144
  183.9 9.5 %multiply_convert_fusion.7 = (bf16[512,1536]{1,0:T(8,128)(2,1)S(1)}, f32[512,1536]{1,0:T(8,128)}, f32[512,1536]{1,0:T(8,128)}) fusion(f32[1536]{0:T(1024)S(1)} %copy-done.111, bf16[768,1536]{1,0:T(8,128)(2,1)S(1)} %copy-done, f32[768]{0:T(1024)S(1)} %copy-done.107, f32[768]{0:T(1024)S(1)} %copy-done.86, f32[512]{0:T(512)S(1)} %fusion.62, ...), kind=kOutput, calls=%fused_computation.42 | convolution fusion | flops 1263403008 | bytes 11815936 | tf_op jit(solution)/shard_map/dot_general | solution.py:148
  194.6 2.3 convolution_convert_fusion.5
  197.0 34.5 %all-reduce.19.cloned.1.call-done = bf16[512,768]{1,0:T(8,128)(2,1)} async-done(((bf16[512,768]{1,0:T(8,128)(2,1)}), bf16[512,768]{1,0:T(8,128)(2,1)}) %all-reduce.19.cloned.1.call-update) | async-done | bytes 786448 | tf_op jit(solution)/shard_map/psum | solution.py:152
  231.5 2.2 fusion.97
  239.0 2.9 convert_reduce_fusion
  243.0 2.3 convolution_convert_fusion.4
  245.4 34.5 %all-reduce.21.cloned.1.call-done = bf16[512,768]{1,0:T(8,128)(2,1)} async-done(((bf16[512,768]{1,0:T(8,128)(2,1)}), bf16[512,768]{1,0:T(8,128)(2,1)}) %all-reduce.21.cloned.1.call-update) | async-done | bytes 786448 | tf_op jit(solution)/shard_map/psum | solution.py:167
  279.8 3.5 multiply_reduce_fusion
  283.4 2.5 fusion.95
  289.8 4.6 convolution_convert_fusion.1
  294.5 4.6 convolution_convert_fusion
  301.2 5.1 convolution_convert_fusion.8
  306.3 5.0 convolution_convert_fusion.9
  311.4 5.2 multiply_convert_fusion
  316.7 6.7 %multiply_convert_fusion.1 = bf16[6,512,512]{1,2,0:T(8,128)(2,1)} fusion(f32[6,512,512]{1,2,0:T(8,128)} %get-tuple-element.191, f32[6,512]{1,0:T(8,128)S(1)} %bitcast.299, f32[6,512]{1,0:T(8,128)S(1)} %log_add_fusion, pred[512,512]{0,1:T(8,128)(4,1)S(1)} %copy-done.57, bf16[512,6,64]{0,2,1:T(8,128)(2,1)S(1)} %bitcast.266, bf16[512,6,64]{0,2,1:T(8,128)(2,1)S(1)} %bitcast.288), kind=kOutput, calls=%fused_computation.1 | convolution fusion | flops 210763776 | bytes 10510336 | tf_op jit(solution)/shard_map/while/body/eval_jaxpr/qhd,khd->hqk/dot_general | solution.py:200
  323.4 2.2 convolution_convert_fusion.10
  325.6 3.9 multiply_convert_fusion.2
  329.6 2.2 convolution_convert_fusion.11
  331.8 4.2 multiply_convert_fusion.4
  337.4 3.9 multiply_convert_fusion.5
  342.9 3.9 multiply_convert_fusion.6
  350.9 3.5 collective-permute-start.11
  355.7 3.0 fusion.41
  359.9 4.2 collective-permute-start.10
  365.3 3.1 fusion.40
  369.7 3.6 collective-permute-start.9
  374.5 3.0 fusion.39
  380.2 3.0 fusion.38
  385.8 3.0 fusion.37
  390.2 3.5 fusion.113
  393.7 5.0 multiply_convert_fusion.3
  403.1 2.3 fusion.83
  408.4 2.3 copy.162
  412.0 3.1 fusion.30
  416.8 10.2 %collective-permute-done.7 = bf16[2,512,384]{2,1,0:T(8,128)(2,1)} collective-permute-done((bf16[2,512,384]{2,1,0:T(8,128)(2,1)}, bf16[2,512,384]{2,1,0:T(8,128)(2,1)}, u32[]{:S(2)}, u32[]{:S(2)}) %collective-permute-start.7) | collective-permute-done | bytes 786464 | tf_op jit(solution)/shard_map/ppermute | solution.py:17
  427.0 3.9 collective-permute-done.6
  431.0 3.4 fusion.22
  434.5 2.4 convolution_convert_fusion.2
  437.4 3.7 bitcast_convert_fusion
  441.2 45.2 %reduce-scatter.5.cloned.1.call-done = bf16[96,3,384]{2,0,1:T(8,128)(2,1)} async-done(((bf16[768,3,384]{2,0,1:T(8,128)(2,1)}), bf16[96,3,384]{2,0,1:T(8,128)(2,1)}) %reduce-scatter.5.cloned.1.call-update) | async-done | bytes 221200 | tf_op jit(solution)/shard_map/reduce_scatter | solution.py:244
  488.0 26.1 %all-reduce.7 = (bf16[768]{0:T(1024)(128)(2,1)S(1)}, bf16[768]{0:T(1024)(128)(2,1)S(1)}, bf16[768]{0:T(1024)(128)(2,1)S(1)}, bf16[768]{0:T(1024)(128)(2,1)S(1)},...) all-reduce(bf16[768]{0:T(1024)(128)(2,1)S(1)} %copy-done.103, ...), channel_id=4, replica_groups=mesh['dp'=2,'seq'=8,'tensor'=2] {'seq'}, use_global_device_ids=true, to_apply=%region_41.42.clone | all-reduce | flops 4608 | bytes 18432
  514.5 4.9 all-reduce.8
  523.9 3.3 fusion.43
  527.2 2.8 fusion.45
  530.1 30.7 %all-reduce.27.cloned.1.call-done = (bf16[96,3,384]{2,0,1:T(8,128)(2,1)}, bf16[96,384]{1,0:T(8,128)(2,1)}, bf16[96,1536]{1,0:T(8,128)(2,1)}, bf16[96,1536]{1,0:T(8,128)(2,1)}) async-done(((bf16[96,3,384]{2,0,1:T(8,128)(2,1)}, bf16[96,384]{1,0:T(8,128)(2,1)}, bf16[96,1536]{1,0:T(8,128)(2,1)}, bf16[96,1536]{1,0:T(8,128)(2,1)}), (bf16[96,3,384]{2,0,1:T(8,128)(2,1)}, bf16[96,384]{1,0:T(8,128)(2,1)}, ...) | async-done | bytes 884752 | tf_op jit(solution)/shard_map/psum | solution.py:276
  567.7 85.4 %all-reduce.25.cloned.1.call-done = (f32[20,768]{1,0:T(8,128)}, f32[384]{0:T(512)}, f32[384]{0:T(512)}, f32[1536]{0:T(1024)}) async-done(((f32[20,768]{1,0:T(8,128)}, f32[384]{0:T(512)}, f32[384]{0:T(512)}, f32[1536]{0:T(1024)}), (f32[20,768]{1,0:T(8,128)}, f32[384]{0:T(512)}, f32[384]{0:T(512)}, f32[1536]{0:T(1024)})) %all-reduce.25.cloned.1.call-update) | async-done | bytes 70672 | tf_op jit(solution)/shard_map/psum | solution.py:287
  (413 shorter events, 115.8 us)
Async XLA Ops:
  7.2 176.7 %copy-start = (bf16[768,1536]{1,0:T(8,128)(2,1)S(1)}, bf16[768,1536]{1,0:T(8,128)(2,1)}, u32[]{:S(2)}) copy-start(bf16[768,1536]{1,0:T(8,128)(2,1)} %param.27) | copy-start | bytes 7077892
  7.2 172.9 %all-reduce.17.cloned.1.call-start = ((), (), s32[]{:S(2)}) async-start(), calls=%async_computation.4 | async-start | bytes 1572864 | tf_op jit(solution)/shard_map/psum | solution.py:144
  16.6 14.9 %copy-start.79 = (s32[1,4096]{1,0:T(1,128)S(1)}, s32[1,4096]{1,0:T(1,128)}, u32[]{:S(2)}) copy-start(s32[1,4096]{1,0:T(1,128)} %param.18) | copy-start | bytes 49156
  18.0 25.3 %collective-permute-start.5 = (bf16[2,512,384]{1,2,0:T(8,128)(2,1)}, bf16[2,512,384]{1,2,0:T(8,128)(2,1)}, u32[]{:S(2)}, u32[]{:S(2)}) collective-permute-start(bf16[2,512,384]{1,2,0:T(8,128)(2,1)} %get-tuple-element.166), channel_id=1, source_target_pairs={{6,0},{8,2},{10,4},{12,6},{14,8},{7,1},{9,3},{11,5},{13,7},{15,9},... | collective-permute-start | bytes 2359304 | tf_op jit(solution)/shard_map/ppermute | solution.py:17
  19.3 31.9 %collective-permute-start.4 = (bf16[2,512,384]{1,2,0:T(8,128)(2,1)}, bf16[2,512,384]{1,2,0:T(8,128)(2,1)}, u32[]{:S(2)}, u32[]{:S(2)}) collective-permute-start(bf16[2,512,384]{1,2,0:T(8,128)(2,1)} %get-tuple-element.166), channel_id=1, source_target_pairs={{4,0},{6,2},{8,4},{10,6},{12,8},{14,10},{5,1},{7,3},{9,5},{11,7},{... | collective-permute-start | bytes 2359304 | tf_op jit(solution)/shard_map/ppermute | solution.py:17
  20.6 32.6 %collective-permute-start.3 = (bf16[2,512,384]{1,2,0:T(8,128)(2,1)}, bf16[2,512,384]{1,2,0:T(8,128)(2,1)}, u32[]{:S(2)}, u32[]{:S(2)}) collective-permute-start(bf16[2,512,384]{1,2,0:T(8,128)(2,1)} %get-tuple-element.166), channel_id=1, source_target_pairs={{2,0},{4,2},{6,4},{8,6},{10,8},{12,10},{14,12},{3,1},{5,3},{7,5},{... | collective-permute-start | bytes 2359304 | tf_op jit(solution)/shard_map/ppermute | solution.py:17
  21.9 33.3 %collective-permute-start.2 = (bf16[2,512,384]{1,2,0:T(8,128)(2,1)}, bf16[2,512,384]{1,2,0:T(8,128)(2,1)}, u32[]{:S(2)}, u32[]{:S(2)}) collective-permute-start(bf16[2,512,384]{1,2,0:T(8,128)(2,1)} %get-tuple-element.166), channel_id=1, source_target_pairs={{0,2},{2,4},{4,6},{6,8},{8,10},{10,12},{12,14},{1,3},{3,5},{5,7},{... | collective-permute-start | bytes 2359304 | tf_op jit(solution)/shard_map/ppermute | solution.py:17
  25.9 31.4 %collective-permute-start.1 = (bf16[2,512,384]{1,2,0:T(8,128)(2,1)}, bf16[2,512,384]{1,2,0:T(8,128)(2,1)}, u32[]{:S(2)}, u32[]{:S(2)}) collective-permute-start(bf16[2,512,384]{1,2,0:T(8,128)(2,1)} %get-tuple-element.166), channel_id=1, source_target_pairs={{0,4},{2,6},{4,8},{6,10},{8,12},{10,14},{1,5},{3,7},{5,9},{7,11},{... | collective-permute-start | bytes 2359304 | tf_op jit(solution)/shard_map/ppermute | solution.py:17
  34.5 32.0 %copy-start.58 = (pred[512,512]{0,1:T(8,128)(4,1)}, pred[512,512]{0,1:T(8,128)(4,1)S(1)}, u32[]{:S(2)}) copy-start(pred[512,512]{0,1:T(8,128)(4,1)S(1)} %get-tuple-element.187) | copy-start | bytes 786436
  34.5 35.8 %copy-start.55 = (pred[512,512]{0,1:T(8,128)(4,1)}, pred[512,512]{0,1:T(8,128)(4,1)S(1)}, u32[]{:S(2)}) copy-start(pred[512,512]{0,1:T(8,128)(4,1)S(1)} %get-tuple-element.186) | copy-start | bytes 786436
  34.5 39.7 %copy-start.22 = (pred[512,512]{0,1:T(8,128)(4,1)}, pred[512,512]{0,1:T(8,128)(4,1)S(1)}, u32[]{:S(2)}) copy-start(pred[512,512]{0,1:T(8,128)(4,1)S(1)} %get-tuple-element.185) | copy-start | bytes 786436
  34.5 40.9 %copy-start.52 = (pred[512,512]{0,1:T(8,128)(4,1)}, pred[512,512]{0,1:T(8,128)(4,1)S(1)}, u32[]{:S(2)}) copy-start(pred[512,512]{0,1:T(8,128)(4,1)S(1)} %get-tuple-element.183) | copy-start | bytes 786436
  34.5 42.1 %copy-start.49 = (pred[512,512]{0,1:T(8,128)(4,1)}, pred[512,512]{0,1:T(8,128)(4,1)S(1)}, u32[]{:S(2)}) copy-start(pred[512,512]{0,1:T(8,128)(4,1)S(1)} %get-tuple-element.182) | copy-start | bytes 786436
  34.6 87.5 %copy-start.20 = (pred[512,512]{0,1:T(8,128)(4,1)}, pred[512,512]{0,1:T(8,128)(4,1)S(1)}, u32[]{:S(2)}) copy-start(pred[512,512]{0,1:T(8,128)(4,1)S(1)} %get-tuple-element.181) | copy-start | bytes 786436
  38.4 79.1 %copy-start.4 = (f32[6,512,512]{1,2,0:T(8,128)}, f32[6,512,512]{1,2,0:T(8,128)S(1)}, u32[]{:S(2)}) copy-start(f32[6,512,512]{1,2,0:T(8,128)S(1)} %get-tuple-element.195) | copy-start | bytes 18874372
  43.4 22.3 %collective-permute-start = (bf16[2,512,384]{1,2,0:T(8,128)(2,1)}, bf16[2,512,384]{1,2,0:T(8,128)(2,1)S(1)}, u32[]{:S(2)}, u32[]{:S(2)}) collective-permute-start(bf16[2,512,384]{1,2,0:T(8,128)(2,1)} %get-tuple-element.166), channel_id=1, source_target_pairs={{0,6},{2,8},{4,10},{6,12},{8,14},{1,7},{3,9},{5,11},{7,13},{9,15},... | collective-permute-start | bytes 2359304 | tf_op jit(solution)/shard_map/ppermute | solution.py:17
  47.4 19.1 %copy-start.37 = (bf16[1,1,512,384]{2,3,1,0:T(8,128)(2,1)}, bf16[1,1,512,384]{2,3,1,0:T(8,128)(2,1)S(1)}, u32[]{:S(2)}) copy-start(bf16[1,1,512,384]{2,3,1,0:T(8,128)(2,1)S(1)} %get-tuple-element.167) | copy-start | bytes 1179652
  53.2 17.1 %copy-start.33 = (bf16[1,1,512,384]{2,3,1,0:T(8,128)(2,1)}, bf16[1,1,512,384]{2,3,1,0:T(8,128)(2,1)S(1)}, u32[]{:S(2)}) copy-start(bf16[1,1,512,384]{2,3,1,0:T(8,128)(2,1)S(1)} %get-tuple-element.164) | copy-start | bytes 1179652
  55.2 18.9 %copy-start.25 = (bf16[1,1,512,384]{2,3,1,0:T(8,128)(2,1)}, bf16[1,1,512,384]{2,3,1,0:T(8,128)(2,1)S(1)}, u32[]{:S(2)}) copy-start(bf16[1,1,512,384]{2,3,1,0:T(8,128)(2,1)S(1)} %get-tuple-element.154) | copy-start | bytes 1179652
  57.3 18.1 %copy-start.35 = (bf16[1,1,512,384]{2,3,1,0:T(8,128)(2,1)}, bf16[1,1,512,384]{2,3,1,0:T(8,128)(2,1)S(1)}, u32[]{:S(2)}) copy-start(bf16[1,1,512,384]{2,3,1,0:T(8,128)(2,1)S(1)} %get-tuple-element.160) | copy-start | bytes 1179652
  59.4 17.3 %copy-start.29 = (bf16[1,1,512,384]{2,3,1,0:T(8,128)(2,1)}, bf16[1,1,512,384]{2,3,1,0:T(8,128)(2,1)S(1)}, u32[]{:S(2)}) copy-start(bf16[1,1,512,384]{2,3,1,0:T(8,128)(2,1)S(1)} %get-tuple-element.158) | copy-start | bytes 1179652
  66.5 11.4 %copy-start.31 = (bf16[1,1,512,384]{2,3,1,0:T(8,128)(2,1)}, bf16[1,1,512,384]{2,3,1,0:T(8,128)(2,1)S(1)}, u32[]{:S(2)}) copy-start(bf16[1,1,512,384]{2,3,1,0:T(8,128)(2,1)S(1)} %get-tuple-element.156) | copy-start | bytes 1179652
  75.4 48.3 %copy-start.3 = (f32[6,512,512]{1,2,0:T(8,128)}, f32[6,512,512]{1,2,0:T(8,128)S(1)}, u32[]{:S(2)}) copy-start(f32[6,512,512]{1,2,0:T(8,128)S(1)} %get-tuple-element.193) | copy-start | bytes 18874372
  76.6 42.4 %copy-start.6 = (f32[6,512,512]{1,2,0:T(8,128)}, f32[6,512,512]{1,2,0:T(8,128)S(1)}, u32[]{:S(2)}) copy-start(f32[6,512,512]{1,2,0:T(8,128)S(1)} %get-tuple-element.197) | copy-start | bytes 18874372
  77.9 42.6 %copy-start.5 = (f32[6,512,512]{1,2,0:T(8,128)}, f32[6,512,512]{1,2,0:T(8,128)S(1)}, u32[]{:S(2)}) copy-start(f32[6,512,512]{1,2,0:T(8,128)S(1)} %get-tuple-element.199) | copy-start | bytes 18874372
  79.1 43.0 %copy-start.2 = (f32[6,512,512]{1,2,0:T(8,128)}, f32[6,512,512]{1,2,0:T(8,128)S(1)}, u32[]{:S(2)}) copy-start(f32[6,512,512]{1,2,0:T(8,128)S(1)} %get-tuple-element.201) | copy-start | bytes 18874372
  80.8 7.6 %copy-start.80 = (f32[6,512]{1,0:T(8,128)}, f32[6,512]{1,0:T(8,128)S(1)}, u32[]{:S(2)}) copy-start(f32[6,512]{1,0:T(8,128)S(1)} %get-tuple-element.142) | copy-start | bytes 36868
  128.6 102.9 %all-reduce.19.cloned.1.call-start = ((), (), s32[]{:S(2)}) async-start(), calls=%async_computation.5 | async-start | bytes 1572864 | tf_op jit(solution)/shard_map/psum | solution.py:152
  181.7 11.8 %copy-start.85 = (f32[512]{0:T(512)}, f32[512]{0:T(512)S(1)}, u32[]{:S(2)}) copy-start(f32[512]{0:T(512)S(1)} %broadcast_multiply_fusion.1) | copy-start | bytes 6148
  183.9 9.6 %copy-start.87 = (f32[512]{0:T(512)}, f32[512]{0:T(512)S(1)}, u32[]{:S(2)}) copy-start(f32[512]{0:T(512)S(1)} %fusion.62) | copy-start | bytes 6148
  183.9 10.7 %copy-start.109 = (bf16[768,1536]{1,0:T(8,128)(2,1)S(1)}, bf16[768,1536]{1,0:T(8,128)(2,1)}, u32[]{:S(2)}) copy-start(bf16[768,1536]{1,0:T(8,128)(2,1)} %param.29) | copy-start | bytes 7077892
  197.0 82.9 %all-reduce.21.cloned.1.call-start = ((), (), s32[]{:S(2)}) async-start(), calls=%async_computation.6 | async-start | bytes 1572864 | tf_op jit(solution)/shard_map/psum | solution.py:167
  245.3 38.1 %copy-start.94 = (f32[512]{0:T(512)S(1)}, f32[512]{0:T(512)}, u32[]{:S(2)}) copy-start(f32[512]{0:T(512)} %copy-done.93) | copy-start | bytes 6148
  245.3 38.1 %copy-start.10 = (bf16[512,768]{1,0:T(8,128)(2,1)S(1)}, bf16[512,768]{1,0:T(8,128)(2,1)}, u32[]{:S(2)}) copy-start(bf16[512,768]{1,0:T(8,128)(2,1)} %all-reduce.17.cloned.1.call-done) | copy-start | bytes 2359300
  245.3 195.9 %reduce-scatter.7.cloned.1.call-start = ((), (), s32[]{:S(2)}) async-start(), calls=%async_computation.9 | async-start | bytes 663552 | tf_op jit(solution)/shard_map/reduce_scatter | solution.py:247
  286.0 8.4 %copy-start.7 = (f32[512,768]{1,0:T(8,128)}, f32[512,768]{1,0:T(8,128)S(1)}, u32[]{:S(2)}) copy-start(f32[512,768]{1,0:T(8,128)S(1)} %get-tuple-element.135) | copy-start | bytes 4718596
  289.8 151.4 %reduce-scatter.9.cloned.1.call-start = ((), (), s32[]{:S(2)}) async-start(), calls=%async_computation.10 | async-start | bytes 2654208 | tf_op jit(solution)/shard_map/reduce_scatter | solution.py:259
  294.4 146.8 %reduce-scatter.11.cloned.1.call-start = ((), (), s32[]{:S(2)}) async-start(), calls=%async_computation.11 | async-start | bytes 2654208 | tf_op jit(solution)/shard_map/reduce_scatter | solution.py:262
  299.1 187.3 %reduce-scatter.5.cloned.1.call-start = ((), (), s32[]{:S(2)}) async-start(), calls=%async_computation.8 | async-start | bytes 1990656 | tf_op jit(solution)/shard_map/reduce_scatter | solution.py:244
  311.4 20.4 %copy-start.96 = (f32[512,6]{0,1:T(8,128)}, f32[512,6]{0,1:T(8,128)S(1)}, u32[]{:S(2)}) copy-start(f32[512,6]{0,1:T(8,128)S(1)} %reduce_sum.288) | copy-start | bytes 36868
  311.4 11.9 %slice-start.2 = ((s8[6291456]{0:T(1024)(128)(4,1)}), s8[4194304]{0:T(1024)(128)(4,1)S(1)}, s32[]{:S(2)}) async-start(s8[6291456]{0:T(1024)(128)(4,1)} %bitcast.225), calls=%async_computation.16 | async-start | bytes 8388608
  316.7 6.7 %slice-start.3 = ((s8[6291456]{0:T(1024)(128)(4,1)}), s8[2097152]{0:T(1024)(128)(4,1)S(1)}, s32[]{:S(2)}) async-start(s8[6291456]{0:T(1024)(128)(4,1)} %bitcast.225), calls=%async_computation.17 | async-start | bytes 4194304
  316.7 6.7 %copy-start.24 = (pred[512,512]{0,1:T(8,128)(4,1)S(1)}, pred[512,512]{0,1:T(8,128)(4,1)}, u32[]{:S(2)}) copy-start(pred[512,512]{0,1:T(8,128)(4,1)} %copy-done.22) | copy-start | bytes 786436
  350.9 54.5 %collective-permute-start.11 = (bf16[2,512,384]{2,1,0:T(8,128)(2,1)}, bf16[2,512,384]{2,1,0:T(8,128)(2,1)}, u32[]{:S(2)}, u32[]{:S(2)}) collective-permute-start(bf16[2,512,384]{2,1,0:T(8,128)(2,1)} %pad_maximum_fusion.7), channel_id=1, source_target_pairs={{0,6},{2,8},{4,10},{6,12},{8,14},{1,7},{3,9},{5,11},{7,13},{9,15},... | collective-permute-start | bytes 2359304 | tf_op jit(solution)/shard_map/ppermute | solution.py:17
  359.9 56.9 %collective-permute-start.10 = (bf16[2,512,384]{2,1,0:T(8,128)(2,1)}, bf16[2,512,384]{2,1,0:T(8,128)(2,1)}, u32[]{:S(2)}, u32[]{:S(2)}) collective-permute-start(bf16[2,512,384]{2,1,0:T(8,128)(2,1)} %pad_maximum_fusion.6), channel_id=1, source_target_pairs={{0,4},{2,6},{4,8},{6,10},{8,12},{10,14},{1,5},{3,7},{5,9},{7,11},{... | collective-permute-start | bytes 2359304 | tf_op jit(solution)/shard_map/ppermute | solution.py:17
  369.7 47.1 %collective-permute-start.9 = (bf16[2,512,384]{2,1,0:T(8,128)(2,1)}, bf16[2,512,384]{2,1,0:T(8,128)(2,1)}, u32[]{:S(2)}, u32[]{:S(2)}) collective-permute-start(bf16[2,512,384]{2,1,0:T(8,128)(2,1)} %pad_maximum_fusion.5), channel_id=1, source_target_pairs={{0,2},{2,4},{4,6},{6,8},{8,10},{10,12},{12,14},{1,3},{3,5},{5,7},{... | collective-permute-start | bytes 2359304 | tf_op jit(solution)/shard_map/ppermute | solution.py:17
  378.7 38.1 %collective-permute-start.8 = (bf16[2,512,384]{2,1,0:T(8,128)(2,1)}, bf16[2,512,384]{2,1,0:T(8,128)(2,1)}, u32[]{:S(2)}, u32[]{:S(2)}) collective-permute-start(bf16[2,512,384]{2,1,0:T(8,128)(2,1)} %pad_maximum_fusion.4), channel_id=1, source_target_pairs={{2,0},{4,2},{6,4},{8,6},{10,8},{12,10},{14,12},{3,1},{5,3},{7,5},{... | collective-permute-start | bytes 2359304 | tf_op jit(solution)/shard_map/ppermute | solution.py:17
  384.4 42.7 %collective-permute-start.7 = (bf16[2,512,384]{2,1,0:T(8,128)(2,1)}, bf16[2,512,384]{2,1,0:T(8,128)(2,1)}, u32[]{:S(2)}, u32[]{:S(2)}) collective-permute-start(bf16[2,512,384]{2,1,0:T(8,128)(2,1)} %pad_maximum_fusion.3), channel_id=1, source_target_pairs={{4,0},{6,2},{8,4},{10,6},{12,8},{14,10},{5,1},{7,3},{9,5},{11,7},{... | collective-permute-start | bytes 2359304 | tf_op jit(solution)/shard_map/ppermute | solution.py:17
  405.4 6.5 copy-start.32
  405.4 25.5 %collective-permute-start.6 = (bf16[2,512,384]{2,1,0:T(8,128)(2,1)}, bf16[2,512,384]{2,1,0:T(8,128)(2,1)}, u32[]{:S(2)}, u32[]{:S(2)}) collective-permute-start(bf16[2,512,384]{2,1,0:T(8,128)(2,1)} %pad_maximum_fusion.2), channel_id=1, source_target_pairs={{6,0},{8,2},{10,4},{12,6},{14,8},{7,1},{9,3},{11,5},{13,7},{15,9},... | collective-permute-start | bytes 2359304 | tf_op jit(solution)/shard_map/ppermute | solution.py:17
  437.0 49.5 %copy-start.17 = (bf16[1,512,768]{2,1,0:T(8,128)(2,1)S(1)}, bf16[1,512,768]{2,1,0:T(8,128)(2,1)}, u32[]{:S(2)}) copy-start(bf16[1,512,768]{2,1,0:T(8,128)(2,1)} %param.33) | copy-start | bytes 2359300
  437.0 49.7 %copy-start.112 = (u32[32]{0:T(128)S(1)}, u32[32]{0:T(128)}, u32[]{:S(2)}) copy-start(u32[32]{0:T(128)} %constant.165) | copy-start | bytes 388
  437.0 50.9 %copy-start.99 = (bf16[768]{0:T(1024)(128)(2,1)S(1)}, bf16[768]{0:T(1024)(128)(2,1)}, u32[]{:S(2)}) copy-start(bf16[768]{0:T(1024)(128)(2,1)} %get-tuple-element.89) | copy-start | bytes 4612
  437.0 50.9 %copy-start.100 = (bf16[768]{0:T(1024)(128)(2,1)S(1)}, bf16[768]{0:T(1024)(128)(2,1)}, u32[]{:S(2)}) copy-start(bf16[768]{0:T(1024)(128)(2,1)} %get-tuple-element.128) | copy-start | bytes 4612
  437.0 50.9 %copy-start.101 = (bf16[768]{0:T(1024)(128)(2,1)S(1)}, bf16[768]{0:T(1024)(128)(2,1)}, u32[]{:S(2)}) copy-start(bf16[768]{0:T(1024)(128)(2,1)} %get-tuple-element.87) | copy-start | bytes 4612
  437.0 50.9 %copy-start.102 = (bf16[768]{0:T(1024)(128)(2,1)S(1)}, bf16[768]{0:T(1024)(128)(2,1)}, u32[]{:S(2)}) copy-start(bf16[768]{0:T(1024)(128)(2,1)} %get-tuple-element.91) | copy-start | bytes 4612
  437.1 50.9 %copy-start.103 = (bf16[768]{0:T(1024)(128)(2,1)S(1)}, bf16[768]{0:T(1024)(128)(2,1)}, u32[]{:S(2)}) copy-start(bf16[768]{0:T(1024)(128)(2,1)} %get-tuple-element.130) | copy-start | bytes 4612
  437.1 86.8 %all-reduce.23.cloned.1.call-start = ((), (), s32[]{:S(2)}) async-start(), calls=%async_computation.7 | async-start | bytes 1572864 | tf_op jit(solution)/shard_map/psum | solution.py:236
  441.1 82.8 %copy-start.90 = (f32[512]{0:T(512)S(1)}, f32[512]{0:T(512)}, u32[]{:S(2)}) copy-start(f32[512]{0:T(512)} %copy-done.89) | copy-start | bytes 6148
  441.1 82.8 %copy-start.92 = (s32[512]{0:T(512)S(1)}, s32[512]{0:T(512)}, u32[]{:S(2)}) copy-start(s32[512]{0:T(512)} %copy-done.91) | copy-start | bytes 6148
  441.1 86.1 %copy-start.105 = (pred[512]{0:T(512)(128)(4,1)S(1)}, pred[512]{0:T(512)(128)(4,1)}, u32[]{:S(2)}) copy-start(pred[512]{0:T(512)(128)(4,1)} %copy-done.104) | copy-start | bytes 1540
  441.1 119.6 %all-reduce.27.cloned.1.call-start = ((), (), s32[]{:S(2)}) async-start(), calls=%async_computation.13 | async-start | bytes 1769472 | tf_op jit(solution)/shard_map/psum | solution.py:276
  486.5 166.7 %all-reduce.25.cloned.1.call-start = ((), (), s32[]{:S(2)}) async-start(), calls=%async_computation.12 | async-start | bytes 172032 | tf_op jit(solution)/shard_map/psum | solution.py:287
  523.9 134.6 %copy-start.1 = (bf16[768,1536]{1,0:T(8,128)(2,1)S(1)}, bf16[768,1536]{1,0:T(8,128)(2,1)}, u32[]{:S(2)}) copy-start(bf16[768,1536]{1,0:T(8,128)(2,1)} %param.27) | copy-start | bytes 7077892
  (85 other events, 274.2 us)
Sparse Core Ops, SparseCore 0:
  128.7 51.3 all-reduce.16
  197.1 34.3 all-reduce.18
  245.4 34.3 all-reduce.20
  289.9 31.4 reduce-scatter.6
  323.6 35.2 reduce-scatter.8
  361.1 54.2 reduce-scatter.10
  437.1 49.2 reduce-scatter.4
  489.3 32.3 all-reduce.22
  524.2 36.5 all-reduce.26
  565.5 87.5 all-reduce.24
where the time goes:
time: 673 us; the launch traced here: 666 us
  waiting for transfers between devices  311 us (46%)
  matrix products  156 us (23%)
  other arithmetic  78.3 us (12%)
  local copies, waits for them, and re-layouts  39.9 us (6%)
  starting transfers between devices  32.1 us (5%)
  blocking collectives  31 us (5%)
  between operations  16.7 us (2%)
    psum x1, waiting for transfers between devices, on_device(): lax.psum((grad_query_bias, grad_value_bias, grad_up_bias, grad_memory), (...  85.4 us
    psum x1, waiting for transfers between devices, on_device(): lax.psum(attn_part.astype(jnp.bfloat16), 'tensor').astype(jnp.float32)  51.5 us
    reduce_scatter x1, waiting for transfers between devices, on_device(): lax.psum_scatter(grad_qkv_weight.astype(jnp.bfloat16), 'seq', scatter_dim...  45.2 us
    psum x1, waiting for transfers between devices, on_device(): lax.psum(down_part.astype(jnp.bfloat16), 'tensor').astype(jnp.float32)  34.5 us
    psum x1, waiting for transfers between devices, on_device(): lax.psum(hidden_part.astype(jnp.bfloat16), 'tensor').astype(jnp.float32)  34.5 us
    dot_general x7, matrix products, backward_block(): jnp.einsum('qhd,khd->hqk', grad_block, value_piece, preferred_element_typ...  32.8 us
    ppermute x12, starting transfers between devices, shifted(): lax.ppermute(value, axis, [(source, source + steps) for source in range(l...  31 us
    psum x1, waiting for transfers between devices, on_device(): lax.psum(reduced[0].astype(jnp.bfloat16), 'dp').astype(jnp.float32)  30.7 us
  transfers between devices with their start and end apart: 22, of which 11 were waited for; matrix products, arithmetic and copies ran while one was open for 23% of the time, Pallas kernels for 0%

commit v1 on v0

v1 whole, which is shorter than its diff:
```python
import functools

import jax
import jax.numpy as jnp
from jax import lax
from jax.experimental import pallas as pl
from jax.experimental.pallas import tpu as pltpu
from jax.sharding import PartitionSpec as P

HEAD_DIM = 64
READ_ROWS = 10
REACH = 3
NORM_EPS = 1e-05
F32, BF16 = jnp.float32, jnp.bfloat16
NT = (((1,), (1,)), ((), ()))
NN = (((1,), (0,)), ((), ()))
NEG = -1e30
FLOOR = -1e29
VMEM = pl.BlockSpec(memory_space=pltpu.VMEM)
SMEM = pl.BlockSpec(memory_space=pltpu.SMEM)


def remote(source, target, send_sem, recv_sem, **where):
    return pltpu.make_async_remote_copy(
        source, target, send_sem, recv_sem, device_id=where, device_id_type=pl.DeviceIdType.MESH
    )


def greet(partners):
    barrier = pltpu.get_barrier_semaphore()
    total = 0
    for present, where in partners:
        total = total + present.astype(jnp.int32)

        @pl.when(present)
        def _():
            pl.semaphore_signal(barrier, inc=1, device_id=where, device_id_type=pl.DeviceIdType.MESH)

    pl.semaphore_wait(barrier, total)


def dot(a, b, dims=NN):
    return lax.dot_general(a, b, dims, preferred_element_type=F32)

def low_half(shape):
    return lax.broadcasted_iota(jnp.int32, shape, len(shape) - 1) < 64

def id_columns(ids_ref, start, count):
    row = jnp.broadcast_to(ids_ref[0:1, pl.ds(start, count)], (128, count))
    return jnp.transpose(row)

def wide(x, count):
    return jnp.concatenate([x] * (count // 128), axis=1)

def split_heads(source_ref, rows, target_ref, pairs, keep):
    for pair in range(pairs):
        block = source_ref[rows, pair * 128:pair * 128 + 128]
        target_ref[2 * pair] = jnp.where(keep, block, jnp.zeros_like(block))
        target_ref[2 * pair + 1] = jnp.where(keep, jnp.zeros_like(block), block)

def sweep(rng_ref, b, body):
    first, full_first, full_last, last = (rng_ref[4 * b + i] for i in range(4))
    lax.fori_loop(full_first, full_last, lambda j, c: body(j, False, c), 0)

    def edge(i, c):
        j = first + i
        return body(jnp.where(j < full_first, j, j + full_last - full_first), True, c)

    lax.fori_loop(0, last - first - (full_last - full_first), edge, 0)

def fwd_kernel(bq, bk, own, rng_ref, q_ref, k_ref, v_ref, ids_ref, o_ref, lse_ref, acc_ref, max_ref, q_heads, cols_ref):
    pairs = q_ref.shape[1] // 128
    rows = q_ref.shape[0]
    low_q, low_k = low_half((bq, 128)), low_half((bk, 128))

    def block(qb, carry):
        mine = pl.ds(pl.multiple_of(qb * bq, bq), bq)
        cols_ref[...] = id_columns(ids_ref, pl.multiple_of(own + qb * bq, bq), bq)
        split_heads(q_ref, mine, q_heads, pairs, low_q)
        acc_ref[...] = jnp.zeros_like(acc_ref)
        max_ref[...] = jnp.full_like(max_ref, FLOOR)

        def step(j, masked, carry):
            there = pl.ds(pl.multiple_of(j * bk, bk), bk)
            def pair_step(pair, carry):
                lanes = pl.ds(pair * 128, 128)
                key = k_ref[there, lanes]
                value = v_ref[there, lanes]
                for odd in range(2):
                    head = 2 * pair + odd
                    scores = dot(q_heads[head], key, NT)
                    if masked:
                        scores = jnp.where(wide(cols_ref[...], bk) == ids_ref[0:1, there], scores, NEG)
                    old = max_ref[head]
                    new = jnp.maximum(old, jnp.max(scores, axis=1, keepdims=True))
                    probs = jnp.exp(scores - wide(new, bk)).astype(BF16)
                    ones = jnp.where(low_k if odd == 0 else ~low_k, value, jnp.ones_like(value))
                    acc_ref[head] = acc_ref[head] * jnp.exp(old - new) + dot(probs, ones)
                    max_ref[head] = new
                return carry
            for pair in range(pairs):
                pair_step(pair, carry)
            return carry

        sweep(rng_ref, qb, step)
        stats = jnp.zeros((bq, 128), F32)
        lane = lax.broadcasted_iota(jnp.int32, (bq, 128), 1)
        for pair in range(pairs):
            even, odd = acc_ref[2 * pair], acc_ref[2 * pair + 1]
            total_even, total_odd = even[:, 64:65], odd[:, 0:1]
            mixed = jnp.where(low_q, even / total_even, odd / total_odd)
            o_ref[mine, pair * 128:pair * 128 + 128] = mixed.astype(BF16)
            stats = jnp.where(lane == 2 * pair, max_ref[2 * pair] + jnp.log(total_even), stats)
            stats = jnp.where(lane == 2 * pair + 1, max_ref[2 * pair + 1] + jnp.log(total_odd), stats)
        lse_ref[mine, :] = stats
        return carry

    lax.fori_loop(0, rows // bq, block, 0)

def attention_forward(rng, query, key, value, ids, own, bq=256, bk=256):
    rows, width = query.shape
    heads = width // 64
    return pl.pallas_call(
        functools.partial(fwd_kernel, bq, bk, own),
        out_shape=(jax.ShapeDtypeStruct((rows, width), BF16), jax.ShapeDtypeStruct((rows, 128), F32)),
        in_specs=[pl.BlockSpec(memory_space=pltpu.SMEM)] + [pl.BlockSpec(memory_space=pltpu.VMEM)] * 4,
        out_specs=(pl.BlockSpec(memory_space=pltpu.VMEM),) * 2,
        scratch_shapes=[pltpu.VMEM((heads, bq, 128), F32), pltpu.VMEM((heads, bq, 128), F32), pltpu.VMEM((heads, bq, 128), BF16), pltpu.VMEM((bq, 128), F32)],
        compiler_params=pltpu.CompilerParams(vmem_limit_bytes=40 << 20),
        name="attention_forward",
    )(rng, query, key, value, ids)

def bwd_kernel(bq, bk, own, rng_ref, q_ref, k_ref, v_ref, g_ref, ids_ref, lse_ref, along_ref, rows_ref, out_ref, dq_acc, dk_acc, dv_acc, q_heads, k_heads, v_heads, g_heads, lse_cols, along_cols, cols_ref):
    rows, width = out_ref.shape[0], q_ref.shape[1]
    pairs = width // 128
    heads = 2 * pairs
    low_q = low_half((bq, 128))

    def block(b, carry):
        start = pl.multiple_of(b * bq, bq)
        mine = pl.ds(start, bq)
        here = pl.ds(pl.multiple_of(own + start, bq), bq)
        cols_ref[...] = id_columns(ids_ref, pl.multiple_of(own + start, bq), bq)
        for source, target in ((q_ref, q_heads), (k_ref, k_heads), (v_ref, v_heads), (g_ref, g_heads)):
            split_heads(source, here, target, pairs, low_q)
        for head in range(heads):
            lse_cols[head] = jnp.broadcast_to(lse_ref[mine, head:head + 1], (bq, 128))
            along_cols[head] = jnp.broadcast_to(along_ref[mine, head:head + 1], (bq, 128))
        for acc in (dq_acc, dk_acc, dv_acc):
            acc[...] = jnp.zeros_like(acc)

        def step(j, masked, carry):
            there = pl.ds(pl.multiple_of(j * bk, bk), bk)
            def pair_step(pair, carry):
                lanes = pl.ds(pair * 128, 128)
                q_far, k_far, v_far, g_far = (r[there, lanes] for r in (q_ref, k_ref, v_ref, g_ref))
                def hide(x):
                    return jnp.where(wide(cols_ref[...], bk) == ids_ref[0:1, there], x, 0.0) if masked else x
                for odd in range(2):
                    head = 2 * pair + odd
                    scores = dot(q_heads[head], k_far, NT)
                    probs = hide(jnp.exp(scores - wide(lse_cols[head], bk)))
                    slope = dot(g_heads[head], v_far, NT)
                    grad = (probs * (slope - wide(along_cols[head], bk))).astype(BF16)
                    dq_acc[head] += dot(grad, k_far)
                    scores = dot(k_heads[head], q_far, NT)
                    probs = hide(jnp.exp(scores - rows_ref[pl.ds(head, 1), there]))
                    slope = dot(v_heads[head], g_far, NT)
                    grad = (probs * (slope - rows_ref[pl.ds(8 + head, 1), there])).astype(BF16)
                    dv_acc[head] += dot(probs.astype(BF16), g_far)
                    dk_acc[head] += dot(grad, q_far)
                return carry
            for pair in range(pairs):
                pair_step(pair, carry)
            return carry

        sweep(rng_ref, b, step)
        for which, (acc, factor) in enumerate(((dq_acc, 0.125), (dk_acc, 1.0), (dv_acc, 1.0))):
            for pair in range(pairs):
                both = jnp.where(low_q, acc[2 * pair], acc[2 * pair + 1]) * factor
                out_ref[mine, which * width + pair * 128:which * width + pair * 128 + 128] = both.astype(BF16)
        return carry

    lax.fori_loop(0, rows // bq, block, 0)

def attention_backward(rng, query, key, value, grads, ids, lse, along, stat_rows, rows, own, bq=256, bk=256):
    width = query.shape[1]
    heads = width // 64
    return pl.pallas_call(
        functools.partial(bwd_kernel, bq, bk, own),
        out_shape=jax.ShapeDtypeStruct((rows, 3 * width), BF16),
        in_specs=[pl.BlockSpec(memory_space=pltpu.SMEM)] + [pl.BlockSpec(memory_space=pltpu.VMEM)] * 8,
        out_specs=pl.BlockSpec(memory_space=pltpu.VMEM),
        scratch_shapes=[pltpu.VMEM((heads, bq, 128), F32)] * 3 + [pltpu.VMEM((heads, bq, 128), BF16)] * 4 + [pltpu.VMEM((heads, bq, 128), F32)] * 2 + [pltpu.VMEM((bq, 128), F32)],
        compiler_params=pltpu.CompilerParams(vmem_limit_bytes=56 << 20),
        name="attention_backward",
    )(rng, query, key, value, grads, ids, lse, along, stat_rows)

def halo_kernel(count, parts, own_ref, window_ref, send_sem, recv_sem, local_sem):
    s = lax.axis_index("seq")
    core = lax.rem(s, 2)
    sibling = s + 1 - 2 * core
    rows = own_ref.shape[0] // parts
    left, right = s >= 2, s < count - 2
    greet(
        [(s >= k, {"seq": s - k}) for k in (1, 2)] + [(s < count - k, {"seq": s + k}) for k in (1, 2)]
    )

    def own(part, kind, slot, target):
        at = pl.ds(part * rows, rows)
        return remote(own_ref.at[at], window_ref.at[slot, at], send_sem.at[kind, part], recv_sem.at[slot, part], seq=target)

    def moved(part, kind, held, slot, target):
        at = pl.ds(part * rows, rows)
        return remote(window_ref.at[held, at], window_ref.at[slot, at], send_sem.at[kind, part], recv_sem.at[slot, part], seq=target)

    def first_copies(part):
        return (
            (right, own(part, 0, 1, s + 2)),
            (left, own(part, 1, 5, s - 2)),
            (core == 0, own(part, 2, 2, sibling)),
            (core == 1, own(part, 2, 4, sibling)),
        )

    def from_left(part):
        return (
            (jnp.logical_and(left, jnp.logical_and(core == 1, right)), moved(part, 3, 1, 0, s + 1)),
            (jnp.logical_and(left, core == 0), moved(part, 4, 1, 0, sibling)),
            (jnp.logical_and(left, core == 1), moved(part, 4, 1, 2, sibling)),
        )

    def from_right(part):
        return (
            (jnp.logical_and(right, jnp.logical_and(core == 0, left)), moved(part, 5, 5, 6, s - 1)),
            (jnp.logical_and(right, core == 0), moved(part, 6, 5, 4, sibling)),
            (jnp.logical_and(right, core == 1), moved(part, 6, 5, 6, sibling)),
        )

    def each(copies, act):
        for present, copy in copies:
            pl.when(present)(functools.partial(act, copy))

    start = lambda copy: copy.start()
    wait_send = lambda copy: copy.wait_send()

    def arrived(slot, part):
        own(part, 0, slot, s).wait_recv()

    for part in range(parts):
        each(first_copies(part), start)
    local = pltpu.make_async_copy(own_ref, window_ref.at[REACH], local_sem)
    local.start()
    for part in range(parts):
        pl.when(left)(functools.partial(arrived, 1, part))
        each(from_left(part), start)
        pl.when(right)(functools.partial(arrived, 5, part))
        each(from_right(part), start)
    local.wait()
    for part in range(parts):
        for slot in (0, 2, 4, 6):
            block = s + slot - REACH
            pl.when(jnp.logical_and(block >= 0, block < count))(functools.partial(arrived, slot, part))
        each(first_copies(part) + from_left(part) + from_right(part), wait_send)


def gather_window(own, count, collective_id, parts=2):
    return pl.pallas_call(
        functools.partial(halo_kernel, count, parts),
        out_shape=jax.ShapeDtypeStruct((2 * REACH + 1,) + own.shape, own.dtype),
        in_specs=[VMEM],
        out_specs=VMEM,
        scratch_shapes=[
            pltpu.SemaphoreType.DMA((7, parts)),
            pltpu.SemaphoreType.DMA((7, parts)),
            pltpu.SemaphoreType.DMA,
        ],
        compiler_params=pltpu.CompilerParams(collective_id=collective_id, has_side_effects=True),
        name="gather_window",
    )(own)


def split_dot(left, right, dims):
    high = right.astype(BF16)
    low = (right - high.astype(F32)).astype(BF16)
    return dot(left, high, dims) + dot(left, low, dims)


def tail_kernel(dps, seqs, chunks, chunk, width, up_ref, down_ref, out_grad_ref, proj_ref, source_ref, weight_ref, input1_ref, select_ref, small_ref,
                up_out, down_out, mix_out, input_out, small_out,
                mix, y_send, y_recv, a_recv, parts, b_recv, mine, c_recv, last, d_recv, small_in, small_recv, small_mine, small_dp,
                y_sems, a_sems, b_sems, c_sems, d_sems, s_sems):
    zs = seqs // 2
    bits = zs.bit_length() - 1
    t, d, s = lax.axis_index("tensor"), lax.axis_index("dp"), lax.axis_index("seq")
    z, core = s // 2, lax.rem(s, 2)
    sibling = s + 1 - 2 * core
    shares = -(-chunk // width)
    owners = small_ref.shape[0]
    block = up_ref.shape[0] // seqs
    rows, columns = proj_ref.shape
    steps = y_send.shape[0]
    span = rows // steps
    true = s >= 0
    partners = [(true, {"seq": lax.rem(s + k, seqs)}) for k in range(1, seqs)]
    partners += [(true, {"dp": lax.rem(d + k, dps)}) for k in range(1, dps)]
    partners += [(true, {"tensor": 1 - t})]
    greet(partners)
    grads = (up_ref, down_ref, mix)
    results = (up_out, down_out, mix_out)
    per = up_ref.shape[1] // chunk

    def piece(c):
        return grads[c // per], (c % per) * chunk

    def a_copy(c, j):
        ref, at = piece(c)
        start = pl.multiple_of((2 * j + 1 - core) * block, 16)
        return remote(ref.at[pl.ds(start, block), pl.ds(at, chunk)], a_recv.at[c, j], a_sems.at[0, c, j], a_sems.at[1, c, j], seq=sibling)

    def b_copy(c, k):
        other = lax.rem(d + k, dps)
        return other, remote(parts.at[c, other], b_recv.at[c, k], b_sems.at[0, c, k], b_sems.at[1, c, k], dp=other)

    def c_copies(c, b):
        size = 2 << b
        high = lax.rem(z // (1 << b), 2)
        partner = z + (1 << b) - (size * high)
        low = lax.rem(partner, size)
        return [
            remote(mine.at[c, i * size + low], c_recv.at[c, (1 << b) * 0 + first_slot(b) + i], c_sems.at[0, c, first_slot(b) + i], c_sems.at[1, c, first_slot(b) + i], seq=2 * partner + core)
            for i in range(zs // size)
        ]

    def first_slot(b):
        return sum(zs // (2 << e) for e in range(b))

    def d_copy(c, k):
        return remote(last.at[c], d_recv.at[c, k], d_sems.at[0, c, k], d_sems.at[1, c, k], dp=lax.rem(d + k, dps))

    def start_a(c):
        for j in range(zs):
            a_copy(c, j).start()

    def end_a(c):
        ref, at = piece(c)
        for j in range(zs):
            a_copy(c, j).wait()
            start = pl.multiple_of((2 * j + core) * block, 16)
            for p in range(shares):
                real = min(width, chunk - p * width)
                lanes = pl.ds(at + p * width, real)
                total = ref[pl.ds(start, block), lanes].astype(F32) + a_recv[c, j, :, p * width:p * width + real].astype(F32)
                parts[c, p, j, :, 0:real] = total.astype(BF16)
                if real < width:
                    parts[c, p, j, :, real:width] = jnp.zeros((block, width - real), BF16)
        for k in range(1, dps):
            other, copy = b_copy(c, k)
            pl.when(other < shares)(copy.start)

    def end_b(c):
        for k in range(1, dps):
            other, copy = b_copy(c, k)
            pl.when(other < shares)(copy.wait_send)

        @pl.when(d < shares)
        def _():
            for k in range(1, dps):
                b_copy(c, k)[1].wait_recv()
            for j in range(zs):
                total = parts[c, d, j].astype(F32)
                for k in range(1, dps):
                    total = total + b_recv[c, k, j].astype(F32)
                mine[c, j] = total.astype(BF16)
            for copy in c_copies(c, 0):
                copy.start()

    def end_c(c, b):
        size = 2 << b
        kept = lax.rem(z, size)

        @pl.when(d < shares)
        def _():
            for i, copy in enumerate(c_copies(c, b)):
                copy.wait()
                held = mine[c, i * size + kept].astype(F32) + c_recv[c, first_slot(b) + i].astype(F32)
                if b < bits - 1:
                    mine[c, i * size + kept] = held.astype(BF16)
                else:
                    last[c] = held.astype(BF16)
            if b < bits - 1:
                for copy in c_copies(c, b + 1):
                    copy.start()
            else:
                for k in range(1, dps):
                    d_copy(c, k).start()

    def end_d(c):
        result = results[c // per]
        at = (c % per) * chunk

        def put(share, value):
            for p in range(shares):
                real = min(width, chunk - p * width)

                @pl.when(share == p)
                def _():
                    result[:, at + p * width:at + p * width + real] = value[:, 0:real].astype(F32)

        @pl.when(d < shares)
        def _():
            put(d, last[c])
            for k in range(1, dps):
                d_copy(c, k).wait_send()
        for k in range(1, dps):
            share = lax.rem(d + dps - k, dps)

            @pl.when(share < shares)
            def _():
                d_copy(c, k).wait_recv()
                put(share, d_recv[c, k])

    stages = [end_a, end_b] + [functools.partial(end_c, b=b) for b in range(bits)] + [end_d]

    def y_copy(i):
        return remote(y_send.at[i], y_recv.at[i], y_sems.at[0, i], y_sems.at[1, i], tensor=1 - t)

    for c in range(2 * per):
        start_a(c)
    for i in range(steps):
        y_send[i] = dot(proj_ref[i * span:(i + 1) * span, :], weight_ref[...], NT).astype(BF16)
        y_copy(i).start()
    out_width = out_grad_ref.shape[1]
    mix[:, 0:out_width] = out_grad_ref[...]
    third = columns // 3
    for i in range(3):
        part = lax.dot_general(source_ref[...], proj_ref[:, i * third:(i + 1) * third], (((0,), (0,)), ((), ())), preferred_element_type=F32)
        mix[:, out_width + i * third:out_width + (i + 1) * third] = part.astype(BF16)
    for c in range(2 * per, chunks):
        start_a(c)
    for i in range(owners):
        small_in[i] = small_ref[i]
    small_in[1, 0:1, 0:third] = jnp.sum(proj_ref[:, 0:third].astype(F32), axis=0, keepdims=True)
    small_in[1, 0:1, third:2 * third] = jnp.sum(proj_ref[:, 2 * third:3 * third].astype(F32), axis=0, keepdims=True)

    def end_y():
        memory = jnp.zeros((32, input_out.shape[1]), F32)
        for i in range(steps):
            y_copy(i).wait()
            at = slice(i * span, (i + 1) * span)
            total = input1_ref[at, :] + (y_send[i].astype(F32) + y_recv[i].astype(F32))
            select = select_ref[at, :]
            memory = memory + split_dot(select, total, (((0,), (0,)), ((), ())))
            inside = dot(select, jnp.ones((32, total.shape[1]), BF16))
            input_out[at, :] = jnp.where(inside > 0.5, 0.0, total).astype(BF16)
        small_in[1, 1:8, :] = memory[0:7]
        small_in[2] = memory[7:15]
        small_in[3, 0:5, :] = memory[15:20]
        for hop in range(1, seqs):
            owner = lax.rem(s + hop, seqs)
            pl.when(owner < owners)(to_owner(hop, owner).start)

    def to_owner(hop, owner):
        return remote(small_in.at[owner], small_recv.at[hop], s_sems.at[0, 0, hop], s_sems.at[1, 0, hop], seq=owner)

    def across(k):
        return remote(small_mine, small_dp.at[k], s_sems.at[0, 1, k], s_sems.at[1, 1, k], dp=lax.rem(d + k, dps))

    def back(hop, owner, target):
        return remote(small_out.at[owner], small_out.at[owner], s_sems.at[0, 2, hop], s_sems.at[1, 2, hop], seq=target)

    def small_one():
        @pl.when(s < owners)
        def _():
            total = small_in[s]
            for hop in range(1, seqs):
                to_owner(hop, s).wait_recv()
                total = total + small_recv[hop]
            small_mine[...] = total
            for k in range(1, dps):
                across(k).start()

    def small_two():
        @pl.when(s < owners)
        def _():
            small_dp[0] = small_mine[...]
            for k in range(1, dps):
                across(k).wait()
            ordered = jnp.zeros(small_mine.shape, F32)
            for index in range(dps):
                ordered = ordered + small_dp[lax.rem(d + dps - index, dps)]
            small_out[s] = ordered
            for hop in range(1, seqs):
                back(hop, s, lax.rem(s + hop, seqs)).start()

    def small_three():
        for hop in range(1, seqs):
            owner = lax.rem(s + hop, seqs)
            pl.when(owner < owners)(to_owner(hop, owner).wait_send)
        for hop in range(1, seqs):
            pl.when(lax.rem(s + seqs - hop, seqs) < owners)(back(hop, 0, s).wait_recv)
            pl.when(s < owners)(back(hop, 0, s).wait_send)

    extra = {2: end_y, 4: small_one, 5: small_two}
    for phase in range(chunks + len(stages) - 1):
        for index in reversed(range(len(stages))):
            c = phase - index
            if 0 <= c < chunks:
                stages[index](c)
        if phase in extra:
            extra[phase]()
    small_three()


def tail(up, down, out, proj, source, weight, input1, select, small, dps, seqs):
    zs = seqs // 2
    dim, hidden = up.shape
    rows = proj.shape[0]
    chunk = hidden // 2
    chunks = 6
    width = -(-chunk // (128 * dps)) * 128
    block = dim // seqs
    steps = 4
    owners = small.shape[0]
    dma = pltpu.SemaphoreType.DMA
    return pl.pallas_call(
        functools.partial(tail_kernel, dps, seqs, chunks, chunk, width),
        out_shape=(
            jax.ShapeDtypeStruct((block, hidden), F32),
            jax.ShapeDtypeStruct((block, hidden), F32),
            jax.ShapeDtypeStruct((block, hidden), F32),
            jax.ShapeDtypeStruct((rows, dim), BF16),
            jax.ShapeDtypeStruct(small.shape, F32),
        ),
        in_specs=[VMEM] * 9,
        out_specs=(VMEM,) * 5,
        scratch_shapes=[
            pltpu.VMEM((dim, hidden), BF16),
            pltpu.VMEM((steps, rows // steps, dim), BF16),
            pltpu.VMEM((steps, rows // steps, dim), BF16),
            pltpu.VMEM((chunks, zs, block, chunk), BF16),
            pltpu.VMEM((chunks, dps, zs, block, width), BF16),
            pltpu.VMEM((chunks, dps, zs, block, width), BF16),
            pltpu.VMEM((chunks, zs, block, width), BF16),
            pltpu.VMEM((chunks, zs - 1, block, width), BF16),
            pltpu.VMEM((chunks, block, width), BF16),
            pltpu.VMEM((chunks, dps, block, width), BF16),
            pltpu.VMEM(small.shape, F32),
            pltpu.VMEM((seqs,) + small.shape[1:], F32),
            pltpu.VMEM(small.shape[1:], F32),
            pltpu.VMEM((dps,) + small.shape[1:], F32),
            dma((2, steps)),
            dma((2, chunks, zs)),
            dma((2, chunks, dps)),
            dma((2, chunks, zs)),
            dma((2, chunks, dps)),
            dma((2, 3, max(seqs, dps))),
        ],
        compiler_params=pltpu.CompilerParams(collective_id=7, has_side_effects=True, vmem_limit_bytes=60 << 20),
        name="tail",
    )(up, down, out, proj, source, weight, input1, select, small)


def memory_slots(id_row):
    count = id_row.shape[0]
    edge = jnp.full((READ_ROWS,), -1, jnp.int32)
    padded = jnp.concatenate([edge, id_row, edge])
    before = sum((padded[READ_ROWS - k:READ_ROWS - k + count] == id_row).astype(jnp.int32) for k in range(1, READ_ROWS + 1))
    behind = sum((padded[READ_ROWS + k:READ_ROWS + k + count] == id_row).astype(jnp.int32) for k in range(1, READ_ROWS + 1))
    return jnp.where(before < READ_ROWS, before, jnp.where(behind < READ_ROWS, 2 * READ_ROWS - 1 - behind, -1))


def document_blocks(id_row, own_ids, window_start, bq, bk):
    table = []
    for b in range(own_ids.shape[0] // bq):
        low, high = own_ids[b * bq], own_ids[b * bq + bq - 1]
        start = jnp.sum((id_row < low).astype(jnp.int32)) - window_start
        end = jnp.sum((id_row <= high).astype(jnp.int32)) - window_start
        first, last = start // bk, (end + bk - 1) // bk
        full_first, full_last = (start + bk - 1) // bk, end // bk
        whole = jnp.logical_and(low == high, full_first < full_last)
        table += [first, jnp.where(whole, full_first, first), jnp.where(whole, full_last, first), last]
    return jnp.stack(table).astype(jnp.int32)


def normalize(hidden, gain, shift):
    centre = jnp.mean(hidden, axis=-1, keepdims=True)
    centred = hidden - centre
    spread = jnp.mean(centred * centred, axis=-1, keepdims=True)
    return centred * lax.rsqrt(spread + NORM_EPS) * gain + shift


def gelu_exact(values):
    return jax.nn.gelu(values, approximate=False)


def column_sums(matrix):
    return jnp.sum(matrix.astype(F32), axis=0)


def on_device(dps, seqs, tokens, doc_ids, memory, qkv_weight, query_bias, value_bias, out_weight, out_bias, norm1_gain, norm1_bias, up_weight, up_bias, down_weight, down_bias, norm2_gain, norm2_bias, out_grad):
    rows = tokens.shape[1]
    width = qkv_weight.shape[2]
    heads = width // HEAD_DIM
    bq, bk = rows, 256
    own = REACH * rows
    pieces = 2 * REACH + 1
    s = lax.axis_index("seq")
    id_row = doc_ids[0]
    edge = jnp.full((own,), -1, jnp.int32)
    window_start = s * rows - own
    slots = memory_slots(id_row)
    window_slots = lax.dynamic_slice_in_dim(jnp.concatenate([edge, slots, edge]), s * rows, pieces * rows, 0)
    window_ids = lax.dynamic_slice_in_dim(jnp.concatenate([edge, id_row, edge]), s * rows, pieces * rows, 0)
    own_ids = window_ids[own:own + rows]
    blocks = document_blocks(id_row, own_ids, window_start, bq, bk)
    ids = jnp.broadcast_to(window_ids.astype(F32)[None], (8, pieces * rows))

    tokens_window = gather_window(tokens[0], seqs, 1).reshape(pieces * rows, -1)
    selector = window_slots[:, None] == jnp.arange(2 * READ_ROWS, dtype=jnp.int32)[None, :]
    memory_rows = jnp.dot(selector.astype(BF16), memory, preferred_element_type=F32).astype(BF16)
    source_window = jnp.where((window_slots >= 0)[:, None], memory_rows, tokens_window)
    projected = jnp.dot(source_window, qkv_weight.reshape(-1, 3 * width), preferred_element_type=F32)
    query = (projected[:, :width] + query_bias).astype(BF16) * 0.125
    key = projected[:, width:2 * width].astype(BF16)
    value = (projected[:, 2 * width:] + value_bias).astype(BF16)
    here = slice(own, own + rows)
    source = source_window[here]
    is_memory = (window_slots[here] >= 0)[:, None]

    mixed_low, logsums = attention_forward(blocks, query[here], key, value, ids, own, bq, bk)

    def both(part):
        low = part.astype(BF16)
        return low.astype(F32) + lax.ppermute(low, "tensor", [(0, 1), (1, 0)]).astype(F32)

    branch = both(jnp.einsum("tf,of->to", mixed_low, out_weight, preferred_element_type=F32)) + out_bias
    first_input = source.astype(F32) + branch
    first_out, first_pull = jax.vjp(normalize, first_input, norm1_gain, norm1_bias)
    first_low = first_out.astype(BF16)
    up_proj = jnp.dot(first_low, up_weight, preferred_element_type=F32) + up_bias
    act_full, gelu_pull = jax.vjp(gelu_exact, up_proj)
    act_low = act_full.astype(BF16)
    down_out = both(jnp.einsum("tf,of->to", act_low, down_weight, preferred_element_type=F32)) + down_bias
    result, second_pull = jax.vjp(normalize, first_out + down_out, norm2_gain, norm2_bias)
    output = result.astype(BF16)[None]
    grad_second, grad_gain2, grad_shift2 = second_pull(out_grad[0].astype(F32))
    down_grad = grad_second.astype(BF16)
    grad_down_weight = jnp.einsum("to,tf->of", down_grad, act_low, preferred_element_type=F32)
    act_grad = jnp.einsum("to,of->tf", down_grad, down_weight, preferred_element_type=F32)
    up_grad = gelu_pull(act_grad)[0].astype(BF16)
    grad_up_weight = jnp.einsum("td,tf->df", first_low, up_grad, preferred_element_type=F32)
    grad_first = grad_second + both(jnp.einsum("tf,df->td", up_grad, up_weight, preferred_element_type=F32))
    grad_input1, grad_gain1, grad_shift1 = first_pull(grad_first)
    branch_grad = grad_input1.astype(BF16)
    grad_out_weight = jnp.einsum("to,tf->of", branch_grad, mixed_low, preferred_element_type=F32)
    mixed_grad = jnp.einsum("to,of->tf", branch_grad, out_weight, preferred_element_type=F32).astype(BF16)
    along = jnp.sum((mixed_grad.astype(F32) * mixed_low.astype(F32)).reshape(rows, heads, HEAD_DIM), axis=-1)

    gap = jnp.zeros((rows, 8 - heads), F32)
    stats = jnp.concatenate([logsums[:, :heads], gap, along, gap], axis=1).T
    grads_window = gather_window(mixed_grad, seqs, 2).reshape(pieces * rows, -1)
    stats_window = gather_window(stats, seqs, 3, 1)
    stats_window = stats_window.transpose(1, 0, 2).reshape(16, pieces * rows)
    along_cols = jnp.pad(along, ((0, 0), (0, 128 - heads)))
    proj_grad = attention_backward(blocks, query, key, value, grads_window, ids, logsums, along_cols, stats_window, rows, own, bq, bk)

    select = jnp.pad(selector[here].astype(BF16), ((0, 0), (0, 12)))
    small = jnp.concatenate([
        jnp.stack([grad_gain1, grad_shift1, grad_gain2, grad_shift2, column_sums(branch_grad), column_sums(down_grad)]),
        column_sums(up_grad).reshape(2, -1), jnp.zeros((24, 2 * width), F32)])
    up_sum, down_sum, mix_sum, input_grad, small = tail(
        grad_up_weight.astype(BF16), grad_down_weight.astype(BF16), grad_out_weight.astype(BF16), proj_grad, source,
        qkv_weight.reshape(-1, 3 * width), grad_input1, select, small.reshape(4, 8, 2 * width), dps, seqs)
    small = small.reshape(32, 2 * width)
    input_grad = input_grad[None]
    piece = small.shape[1] // seqs
    vectors = lax.dynamic_slice_in_dim(small[:6], s * piece, piece, 1)
    memory_grad = small[9:29]
    return (
        output, input_grad, memory_grad,
        mix_sum[:, width:].reshape(-1, 3, width), small[8, :width], small[8, width:],
        mix_sum[:, :width], vectors[4], vectors[0], vectors[1],
        up_sum, small[6:8].reshape(-1), down_sum, vectors[5], vectors[2], vectors[3],
    )


def solution(mesh):
    in_specs = (
        P("dp", "seq", None), P("dp", None), P(), P(None, None, "tensor"), P("tensor"), P("tensor"), P(None, "tensor"), P(), P(), P(),
        P(None, "tensor"), P("tensor"), P(None, "tensor"), P(), P(), P(), P("dp", "seq", None),
    )
    out_specs = (
        P("dp", "seq", None), P("dp", "seq", None), P(), P("seq", None, "tensor"), P("tensor"), P("tensor"), P("seq", "tensor"), P("seq"), P("seq"), P("seq"),
        P("seq", "tensor"), P("tensor"), P("seq", "tensor"), P("seq"), P("seq"), P("seq"),
    )
    step = functools.partial(on_device, mesh.shape["dp"], mesh.shape["seq"])
    return jax.shard_map(step, mesh=mesh, in_specs=in_specs, out_specs=out_specs, check_vma=False)
```

time: 673 us -> 345 us (0.51)
  waiting for transfers between devices: 311 us -> 13 us
  Pallas kernels: 0 us -> 197 us
  matrix products: 156 us -> 37.5 us
  other arithmetic: 78.3 us -> 42.3 us
  blocking collectives: 31 us -> 0 us
  starting transfers between devices: 32.1 us -> 3.68 us
  between operations: 16.7 us -> 4.38 us
    psum x6 -> x0, waiting for transfers between devices: 237 us -> none  [the longest x1 85.4 us: on_device(): lax.psum((grad_query_bias, grad_value_bias, grad_up_bias, grad_memory), (...]
    pallas_call x0 -> x6, Pallas kernels: none -> 197 us  [the longest x1 102 us: tail(): pl.pallas_call(functools.partial(tail_kernel, dps, seqs, chunks, chunk, w...]
    dot_general x56 -> x11, matrix products: 156 us -> 37.5 us  [the longest x1 7.87 us: on_device(): jnp.dot(first_low, up_weight, preferred_element_type=F32) + up_bias]
    reduce_scatter x4 -> x0, waiting for transfers between devices: 45.2 us -> none  [the longest x1 45.2 us: on_device(): lax.psum_scatter(grad_qkv_weight.astype(jnp.bfloat16), 'seq', scatter_dim...]
    ppermute x12 -> x3, starting transfers between devices: 31 us -> 3.68 us  [both(): lax.ppermute(low, 'tensor', [(0, 1), (1, 0)]).astype(F32)]
    unnamed x1 -> x0, blocking collectives: 26.1 us -> none
    reduce_sum x15 -> x8, other arithmetic: 35.3 us -> 9.85 us  [the longest x1 3.56 us: document_blocks(): start = jnp.sum((id_row < low).astype(jnp.int32)) - window_start]
    ppermute x12 -> x3, waiting for transfers between devices: 29.2 us -> 13 us  [both(): lax.ppermute(low, 'tensor', [(0, 1), (1, 0)]).astype(F32)]
  transfers between devices with their start and end apart: 22 -> 3, of which waited for: 11 -> 1; matrix products, arithmetic and copies ran while one was open for 23% -> 10% of each run, Pallas kernels for 0% -> 0%
where the time goes in v1:
time: 345 us; the launch traced here: 339 us
  Pallas kernels  197 us (57%)
  other arithmetic  42.3 us (12%)
  local copies, waits for them, and re-layouts  41.6 us (12%)
  matrix products  37.5 us (11%)
  waiting for transfers between devices  13 us (4%)
  between operations  4.38 us (1%)
  starting transfers between devices  3.68 us (1%)
    pallas_call x1, Pallas kernels, tail(): pl.pallas_call(functools.partial(tail_kernel, dps, seqs, chunks, chunk, w...  102 us
    pallas_call x3, Pallas kernels, gather_window(): pl.pallas_call(functools.partial(halo_kernel, count, parts), out_shape=ja...  65.6 us
    pallas_call x1, Pallas kernels, attention_backward(): pl.pallas_call(functools.partial(bwd_kernel, bq, bk, own), out_shape=jax....  21.8 us
    unnamed x84, local copies, waits for them, and re-layouts  18.5 us
    eq x1, other arithmetic, on_device(): window_slots[:, None] == jnp.arange(2 * READ_ROWS, dtype=jnp.int32)[None, :]  16.2 us
    ppermute x3, waiting for transfers between devices, both(): lax.ppermute(low, 'tensor', [(0, 1), (1, 0)]).astype(F32)  13 us
    dot_general x1, matrix products, on_device(): jnp.dot(first_low, up_weight, preferred_element_type=F32) + up_bias  7.87 us
    pallas_call x1, Pallas kernels, attention_forward(): pl.pallas_call(functools.partial(fwd_kernel, bq, bk, own), out_shape=(jax...  7.63 us
  transfers between devices with their start and end apart: 3, of which 1 were waited for; matrix products, arithmetic and copies ran while one was open for 10% of the time, Pallas kernels for 0%

profile of v1, /device:TPU:0, one launch (start us, length us, event | category | flops | bytes accessed | tf_op | source)
XLA Modules:
  0.0 339.3 jit_solution(17485922042971690433)
XLA Ops:
  0.7 1.0 fusion.53
  1.6 0.6 fusion.57
  3.5 3.6 %convert_reduce_fusion.5 = (s32[]{:T(128)}, s32[]{:T(128)}, s32[4096]{0:T(1024)S(1)}) fusion(s32[4096]{0:T(1024)} %bitcast.91, s32[]{:T(128)} %bitcast.3, s32[]{:T(128)} %bitcast.5), kind=kLoop, calls=%fused_computation.114 | loop fusion | flops 282622 | bytes 32784 | tf_op jit(solution)/shard_map/reduce_sum | solution.py:576
  8.6 3.8 %copy.48 = bf16[768,3,384]{0,2,1:T(8,128)(2,1)} copy(bf16[768,3,384]{2,0,1:T(8,128)(2,1)} %param.20) | data formatting | bytes 3538944 | tf_op args[3]
  12.4 27.6 %gather_window.3 = bf16[7,512,768]{2,1,0:T(8,128)(2,1)} custom-call(bf16[512,768]{1,0:T(8,128)(2,1)} %bitcast.82), custom_call_target="tpu_custom_call" | custom-call | tf_op jit(solution)/shard_map/gather_window/pallas_call | solution.py:267
  40.1 6.1 %fusion = bf16[3584,768]{1,0:T(8,128)(2,1)S(1)} fusion(bf16[3584,768]{1,0:T(8,128)(2,1)} %bitcast.74, bf16[20,768]{1,0:T(8,128)(2,1)S(1)} %copy-done.24, pred[3584]{0:T(1024)(128)(4,1)S(1)} %get-tuple-element.106, s32[3584]{0:T(1024)S(1)} %get-tuple-element.107), kind=kOutput, calls=%fused_computation.1 | convolution fusion | flops 115677184 | bytes 11058688 | tf_op jit(solution)/shard_map/dot_general | solution.py:620
  46.2 7.4 %fusion.58 = f32[3584,1152]{1,0:T(8,128)S(1)} fusion(bf16[3584,768]{1,0:T(8,128)(2,1)S(1)} %fusion, bf16[768,1152]{0,1:T(8,128)(2,1)S(1)} %bitcast.77), kind=kOutput, calls=%fused_computation.146 | convolution fusion | flops 6341787648 | bytes 23789568 | tf_op jit(solution)/shard_map/dot_general | solution.py:622
  53.6 5.7 %copy-done.13 = f32[3584,1152]{1,0:T(8,128)} copy-done((f32[3584,1152]{1,0:T(8,128)}, f32[3584,1152]{1,0:T(8,128)S(1)}, u32[]{:S(2)}) %copy-start.13) | copy-done | bytes 16515096
  59.2 2.1 fusion.1.v_ref
  61.4 6.5 %fusion.56 = (bf16[3584,384]{1,0:T(8,128)(2,1)}, bf16[3584,384]{1,0:T(8,128)(2,1)S(1)}) fusion(f32[3584,1152]{1,0:T(8,128)} %copy-done.13, f32[384]{0:T(512)S(1)} %copy-done.36), kind=kLoop, calls=%fused_computation.144 | loop fusion | flops 4128768 | bytes 13764096 | tf_op jit(solution)/shard_map/slice | solution.py:624
  67.8 1.5 copy-done.12
  69.5 1.8 copy-done.1
  71.3 1.8 copy-done.2
  73.1 7.6 %attention_forward.1 = (bf16[512,384]{1,0:T(8,128)(2,1)S(1)}, f32[512,128]{1,0:T(8,128)S(1)}) custom-call(s32[4]{0:T(128)S(1)} %pad_add_fusion.rng_ref, bf16[512,384]{1,0:T(8,128)(2,1)S(1)} %slice.196.q_ref, bf16[3584,384]{1,0:T(8,128)(2,1)S(1)} %copy-done.2, bf16[3584,384]{1,0:T(8,128)(2,1)S(1)} %copy-done.1, f32[8,3584]{1,0:T(8,128)S(1)} %broadcast_in_dim.35.ids_ref), custom_call_target="tpu_custom_call" | custom-call | tf_op jit(solution)/shard_map/attention_forward/pallas_call | solution.py:123
  80.8 0.6 convolution_convert_fusion.5
  81.4 1.6 collective-permute-start
  83.0 13.0 %collective-permute-done = bf16[512,768]{1,0:T(8,128)(2,1)S(1)} collective-permute-done((bf16[512,768]{1,0:T(8,128)(2,1)S(1)}, bf16[512,768]{1,0:T(8,128)(2,1)S(1)}, u32[]{:S(2)}, u32[]{:S(2)}) %collective-permute-start) | collective-permute-done | bytes 786464 | tf_op jit(solution)/shard_map/ppermute | solution.py:634
  96.0 1.6 fusion.52
  97.9 7.9 %multiply_convert_fusion = (bf16[512,1536]{1,0:T(8,128)(2,1)S(1)}, f32[512,1536]{1,0:T(8,128)S(1)}, f32[512,1536]{1,0:T(8,128)S(1)}) fusion(f32[1536]{0:T(1024)S(1)} %copy-done.38, bf16[768,1536]{1,0:T(8,128)(2,1)S(1)} %copy-done, f32[512,768]{1,0:T(8,128)S(1)} %get-tuple-element.103, f32[768]{0:T(1024)S(1)} %copy-done.34, f32[768]{0:T(1024)S(1)} %copy-done.25, ...), kind=kOutput, calls=%fused_computation.14 | convolution fusion | flops 1261830144 | bytes 11812864 | tf_op jit(solution)/shard_map/dot_general | solution.py:640
  105.9 1.4 convolution_convert_fusion.4
  107.3 1.6 collective-permute-start.1
  108.9 16.2 %iota_compare_fusion = pred[3584,20]{1,0:T(8,128)(4,1)S(1)} fusion(s32[3584]{0:T(1024)S(1)} %get-tuple-element.107), kind=kLoop, calls=%fused_computation.37 | loop fusion | flops 71680 | bytes 86016 | tf_op jit(solution)/shard_map/eq | solution.py:619
  125.3 0.7 fusion.50
  126.4 0.8 fusion.15
  127.2 1.6 fusion.49
  129.0 1.4 fusion.59
  130.4 1.4 convert_reduce_fusion
  131.9 2.3 convolution_convert_fusion.3
  134.2 0.5 collective-permute-start.2
  134.7 0.7 pad_convert_fusion.select_ref
  135.4 3.8 %copy.54.weight_ref = bf16[768,1152]{1,0:T(8,128)(2,1)} copy(bf16[768,1152]{0,1:T(8,128)(2,1)} %bitcast.76) | data formatting | bytes 3538944 | tf_op jit(solution)/shard_map/reshape | solution.py:622
  139.2 2.1 slice.192.source_ref
  141.3 0.6 reshape.152
  142.0 0.6 reshape.151
  142.6 0.6 stack.31
  143.2 0.6 reshape.153
  143.8 4.6 %convolution_convert_fusion.1.down_ref = bf16[768,1536]{1,0:T(8,128)(2,1)} fusion(bf16[512,768]{1,0:T(8,128)(2,1)} %copy-done.20, bf16[512,1536]{1,0:T(8,128)(2,1)} %copy-done.39), kind=kOutput, calls=%fused_computation.8 | convolution fusion | flops 1209139200 | bytes 4718592 | tf_op jit(solution)/shard_map/to,tf->of/dot_general | solution.py:648
  148.4 3.1 convolution_convert_fusion.2.up_ref
  151.6 2.3 multiply_reduce_fusion
  153.9 0.6 fusion.48
  154.8 1.4 convolution_convert_fusion.6.out_grad_ref
  156.2 1.3 convert_multiply_fusion
  157.6 1.1 copy.50
  158.7 1.2 reduce_sum.175
  160.1 0.6 maximum_bitcast_fusion.own_ref
  160.7 21.8 %gather_window.5 = f32[7,16,512]{2,1,0:T(8,128)} custom-call(f32[16,512]{1,0:T(8,128)} %maximum_bitcast_fusion.own_ref), custom_call_target="tpu_custom_call" | custom-call | tf_op jit(solution)/shard_map/gather_window/pallas_call | solution.py:267
  182.5 1.7 copy.59
  184.2 0.7 pad.30.along_ref
  184.9 16.2 %gather_window.4 = bf16[7,512,384]{2,1,0:T(8,128)(2,1)} custom-call(bf16[512,384]{1,0:T(8,128)(2,1)} %get-tuple-element.122.own_ref), custom_call_target="tpu_custom_call" | custom-call | tf_op jit(solution)/shard_map/gather_window/pallas_call | solution.py:267
  201.2 21.8 %attention_backward.1.proj_ref = bf16[512,1152]{1,0:T(8,128)(2,1)} custom-call(s32[4]{0:T(128)} %copy-done.5, bf16[3584,384]{1,0:T(8,128)(2,1)} %copy-done.12, bf16[3584,384]{1,0:T(8,128)(2,1)} %get-tuple-element.108.k_ref, bf16[3584,384]{1,0:T(8,128)(2,1)} %fusion.1.v_ref, bf16[3584,384]{1,0:T(8,128)(2,1)} %bitcast.75, f32[8,3584]{1,0:T(8,128)} %copy-done.4, ...), custom_call_target="tpu_custom_call" | custom-call | tf_op jit(solution)/shard_map/attention_backward/pallas_call | solution.py:189
  223.0 1.3 concatenate.42
  224.3 102.0 %tail.1 = (f32[96,1536]{1,0:T(8,128)}, f32[96,1536]{1,0:T(8,128)}, f32[96,1536]{1,0:T(8,128)}, bf16[512,768]{1,0:T(8,128)(2,1)}, f32[4,8,768]{2,1,0:T(8,128)}) custom-call(bf16[768,1536]{1,0:T(8,128)(2,1)} %convolution_convert_fusion.2.up_ref, bf16[768,1536]{1,0:T(8,128)(2,1)} %convolution_convert_fusion.1.down_ref, ...), custom_call_target="tpu_custom_call" | custom-call | tf_op jit(solution)/shard_map/tail/pallas_call | solution.py:525
  326.2 1.3 slice_reduce_fusion
  327.5 0.7 slice.204
  328.3 0.7 slice.203
  329.0 1.5 slice.200
  330.6 1.6 slice.183
  332.1 1.1 slice.180
  333.2 0.6 reshape.157
  333.9 0.5 slice_bitcast_fusion
  334.5 0.8 copy.61
  335.3 2.1 copy.65
  337.3 0.8 copy.66
  338.1 0.8 copy.67
  (106 shorter events, 2.0 us)
Async XLA Ops:
  0.6 97.3 %copy-start = (bf16[768,1536]{1,0:T(8,128)(2,1)S(1)}, bf16[768,1536]{1,0:T(8,128)(2,1)}, u32[]{:S(2)}) copy-start(bf16[768,1536]{1,0:T(8,128)(2,1)} %param.27) | copy-start | bytes 7077892
  12.4 27.6 %copy-start.24 = (bf16[20,768]{1,0:T(8,128)(2,1)S(1)}, bf16[20,768]{1,0:T(8,128)(2,1)}, u32[]{:S(2)}) copy-start(bf16[20,768]{1,0:T(8,128)(2,1)} %param.19) | copy-start | bytes 92164
  40.0 6.1 %copy-start.14 = (bf16[768,3,384]{0,2,1:T(8,128)(2,1)S(1)}, bf16[768,3,384]{0,2,1:T(8,128)(2,1)}, u32[]{:S(2)}) copy-start(bf16[768,3,384]{0,2,1:T(8,128)(2,1)} %copy.48) | copy-start | bytes 5308420
  46.1 7.4 %copy-start.9 = (bf16[3584,768]{1,0:T(8,128)(2,1)}, bf16[3584,768]{1,0:T(8,128)(2,1)S(1)}, u32[]{:S(2)}) copy-start(bf16[3584,768]{1,0:T(8,128)(2,1)S(1)} %fusion) | copy-start | bytes 16515076
  46.2 13.0 %copy-start.35 = (f32[384]{0:T(512)S(1)}, f32[384]{0:T(512)}, u32[]{:S(2)}) copy-start(f32[384]{0:T(512)} %param.22) | copy-start | bytes 4612
  53.5 5.7 %copy-start.13 = (f32[3584,1152]{1,0:T(8,128)}, f32[3584,1152]{1,0:T(8,128)S(1)}, u32[]{:S(2)}) copy-start(f32[3584,1152]{1,0:T(8,128)S(1)} %fusion.58) | copy-start | bytes 49545220
  59.2 2.1 copy-start.36
  67.8 1.5 copy-start.12
  69.5 11.3 %copy-start.5 = (s32[4]{0:T(128)}, s32[4]{0:T(128)S(1)}, u32[]{:S(2)}) copy-start(s32[4]{0:T(128)S(1)} %pad_add_fusion.rng_ref) | copy-start | bytes 52
  69.5 11.3 %copy-start.4 = (f32[8,3584]{1,0:T(8,128)}, f32[8,3584]{1,0:T(8,128)S(1)}, u32[]{:S(2)}) copy-start(f32[8,3584]{1,0:T(8,128)S(1)} %broadcast_in_dim.35.ids_ref) | copy-start | bytes 344068
  69.5 1.8 copy-start.1
  71.3 1.8 copy-start.2
  73.1 7.7 %copy-start.16 = (bf16[768,384]{1,0:T(8,128)(2,1)S(1)}, bf16[768,384]{1,0:T(8,128)(2,1)}, u32[]{:S(2)}) copy-start(bf16[768,384]{1,0:T(8,128)(2,1)} %param.23) | copy-start | bytes 1769476
  73.1 22.9 %copy-start.32 = (f32[768]{0:T(1024)S(1)}, f32[768]{0:T(1024)}, u32[]{:S(2)}) copy-start(f32[768]{0:T(1024)} %param.24) | copy-start | bytes 9220
  80.8 61.1 %copy-start.3 = (f32[512,128]{1,0:T(8,128)}, f32[512,128]{1,0:T(8,128)S(1)}, u32[]{:S(2)}) copy-start(f32[512,128]{1,0:T(8,128)S(1)} %get-tuple-element.24.lse_ref) | copy-start | bytes 786436
  81.4 16.5 %copy-start.25 = (f32[768]{0:T(1024)S(1)}, f32[768]{0:T(1024)}, u32[]{:S(2)}) copy-start(f32[768]{0:T(1024)} %param.25) | copy-start | bytes 9220
  81.4 16.5 %copy-start.34 = (f32[768]{0:T(1024)S(1)}, f32[768]{0:T(1024)}, u32[]{:S(2)}) copy-start(f32[768]{0:T(1024)} %param.26) | copy-start | bytes 9220
  81.4 16.5 %copy-start.38 = (f32[1536]{0:T(1024)S(1)}, f32[1536]{0:T(1024)}, u32[]{:S(2)}) copy-start(f32[1536]{0:T(1024)} %param.28) | copy-start | bytes 18436
  81.4 14.5 %collective-permute-start = (bf16[512,768]{1,0:T(8,128)(2,1)S(1)}, bf16[512,768]{1,0:T(8,128)(2,1)S(1)}, u32[]{:S(2)}, u32[]{:S(2)}) collective-permute-start(bf16[512,768]{1,0:T(8,128)(2,1)S(1)} %convolution_convert_fusion.5), channel_id=1, source_target_pairs={{0,1},{1,0},{2,3},{3,2},{4,5},{5,4},{6,7},{7,6},{8,9},{9,8},{10,11... | collective-permute-start | bytes 2359304 | tf_op jit(solution)/shard_map/ppermute | solution.py:634
  97.6 27.7 %copy-start.6 = (f32[512,768]{1,0:T(8,128)}, f32[512,768]{1,0:T(8,128)S(1)}, u32[]{:S(2)}) copy-start(f32[512,768]{1,0:T(8,128)S(1)} %get-tuple-element.103) | copy-start | bytes 4718596
  97.9 7.9 %copy-start.37 = (bf16[768,1536]{1,0:T(8,128)(2,1)S(1)}, bf16[768,1536]{1,0:T(8,128)(2,1)}, u32[]{:S(2)}) copy-start(bf16[768,1536]{1,0:T(8,128)(2,1)} %param.29) | copy-start | bytes 7077892
  105.8 1.5 copy-start.39
  105.8 19.3 %copy-start.15 = (bf16[1,512,768]{2,1,0:T(8,128)(2,1)S(1)}, bf16[1,512,768]{2,1,0:T(8,128)(2,1)}, u32[]{:S(2)}) copy-start(bf16[1,512,768]{2,1,0:T(8,128)(2,1)} %param.33) | copy-start | bytes 2359300
  105.9 19.5 %copy-start.33 = (f32[768]{0:T(1024)S(1)}, f32[768]{0:T(1024)}, u32[]{:S(2)}) copy-start(f32[768]{0:T(1024)} %param.30) | copy-start | bytes 9220
  107.3 18.0 %collective-permute-start.1 = (bf16[512,768]{1,0:T(8,128)(2,1)S(1)}, bf16[512,768]{1,0:T(8,128)(2,1)S(1)}, u32[]{:S(2)}, u32[]{:S(2)}) collective-permute-start(bf16[512,768]{1,0:T(8,128)(2,1)S(1)} %convolution_convert_fusion.4), channel_id=1, source_target_pairs={{0,1},{1,0},{2,3},{3,2},{4,5},{5,4},{6,7},{7,6},{8,9},{9,8},{10,11... | collective-permute-start | bytes 2359304 | tf_op jit(solution)/shard_map/ppermute | solution.py:634
  125.1 0.9 copy-start.21
  125.3 1.1 copy-start.27
  126.0 1.1 copy-start.31
  128.8 1.6 copy-start.10
  129.0 1.4 copy-start.20
  131.8 2.3 copy-start.18
  131.8 2.8 slice-start
  134.2 17.4 %collective-permute-start.2 = (bf16[512,768]{1,0:T(8,128)(2,1)}, bf16[512,768]{1,0:T(8,128)(2,1)}, u32[]{:S(2)}, u32[]{:S(2)}) collective-permute-start(bf16[512,768]{1,0:T(8,128)(2,1)} %convolution_convert_fusion.3), channel_id=1, source_target_pairs={{0,1},{1,0},{2,3},{3,2},{4,5},{5,4},{6,7},{7,6},{8,9},{9,8},{10,11... | collective-permute-start | bytes 2359304 | tf_op jit(solution)/shard_map/ppermute | solution.py:634
  143.8 4.6 %copy-start.7 = (f32[512,768]{1,0:T(8,128)S(1)}, f32[512,768]{1,0:T(8,128)}, u32[]{:S(2)}) copy-start(f32[512,768]{1,0:T(8,128)} %copy-done.6) | copy-start | bytes 4718596
  143.8 4.6 %copy-start.19 = (bf16[512,1536]{1,0:T(8,128)(2,1)S(1)}, bf16[512,1536]{1,0:T(8,128)(2,1)}, u32[]{:S(2)}) copy-start(bf16[512,1536]{1,0:T(8,128)(2,1)} %copy-done.18) | copy-start | bytes 4718596
  148.4 3.1 copy-start.11
  154.6 1.7 copy-start.17
  154.8 2.8 copy-start.8
  201.1 21.8 %copy-start.26 = (f32[2,768]{1,0:T(2,128)S(1)}, f32[2,768]{1,0:T(2,128)}, u32[]{:S(2)}) copy-start(f32[2,768]{1,0:T(2,128)} %reshape.153) | copy-start | bytes 18436
  201.1 21.8 %copy-start.28 = (f32[1,768]{1,0:T(1,128)S(1)}, f32[1,768]{1,0:T(1,128)}, u32[]{:S(2)}) copy-start(f32[1,768]{1,0:T(1,128)} %reshape.152) | copy-start | bytes 9220
  201.1 21.8 %copy-start.29 = (f32[1,768]{1,0:T(1,128)S(1)}, f32[1,768]{1,0:T(1,128)}, u32[]{:S(2)}) copy-start(f32[1,768]{1,0:T(1,128)} %reshape.151) | copy-start | bytes 9220
  201.2 21.8 %copy-start.30 = (f32[1,768]{1,0:T(1,128)S(1)}, f32[1,768]{1,0:T(1,128)}, u32[]{:S(2)}) copy-start(f32[1,768]{1,0:T(1,128)} %stack.31) | copy-start | bytes 9220
  332.1 6.0 %copy-start.22 = (f32[96,1536]{1,0:T(8,128)S(1)}, f32[96,1536]{1,0:T(8,128)}, u32[]{:S(2)}) copy-start(f32[96,1536]{1,0:T(8,128)} %get-tuple-element.151) | copy-start | bytes 1769476
  333.8 3.5 %copy-start.23 = (f32[96,1536]{1,0:T(8,128)S(1)}, f32[96,1536]{1,0:T(8,128)}, u32[]{:S(2)}) copy-start(f32[96,1536]{1,0:T(8,128)} %get-tuple-element.149) | copy-start | bytes 1769476

commit v2 on v1

--- a/solution.py
+++ b/solution.py
@@ -70,13 +70,13 @@
 
 def fwd_kernel(bq, bk, own, rng_ref, q_ref, k_ref, v_ref, ids_ref, o_ref, lse_ref, acc_ref, max_ref, q_heads, cols_ref):
     pairs = q_ref.shape[1] // 128
-    rows = q_ref.shape[0]
+    rows = o_ref.shape[0]
     low_q, low_k = low_half((bq, 128)), low_half((bk, 128))
 
     def block(qb, carry):
         mine = pl.ds(pl.multiple_of(qb * bq, bq), bq)
         cols_ref[...] = id_columns(ids_ref, pl.multiple_of(own + qb * bq, bq), bq)
-        split_heads(q_ref, mine, q_heads, pairs, low_q)
+        split_heads(q_ref, pl.ds(pl.multiple_of(own + qb * bq, bq), bq), q_heads, pairs, low_q)
         acc_ref[...] = jnp.zeros_like(acc_ref)
         max_ref[...] = jnp.full_like(max_ref, FLOOR)
 
@@ -117,8 +117,8 @@
 
     lax.fori_loop(0, rows // bq, block, 0)
 
-def attention_forward(rng, query, key, value, ids, own, bq=256, bk=256):
-    rows, width = query.shape
+def attention_forward(rng, query, key, value, ids, rows, own, bq=256, bk=256):
+    width = query.shape[1]
     heads = width // 64
     return pl.pallas_call(
         functools.partial(fwd_kernel, bq, bk, own),
@@ -126,7 +126,7 @@
         in_specs=[pl.BlockSpec(memory_space=pltpu.SMEM)] + [pl.BlockSpec(memory_space=pltpu.VMEM)] * 4,
         out_specs=(pl.BlockSpec(memory_space=pltpu.VMEM),) * 2,
         scratch_shapes=[pltpu.VMEM((heads, bq, 128), F32), pltpu.VMEM((heads, bq, 128), F32), pltpu.VMEM((heads, bq, 128), BF16), pltpu.VMEM((bq, 128), F32)],
-        compiler_params=pltpu.CompilerParams(vmem_limit_bytes=40 << 20),
+        compiler_params=pltpu.CompilerParams(vmem_limit_bytes=24 << 20),
         name="attention_forward",
     )(rng, query, key, value, ids)
 
@@ -192,91 +192,218 @@
         in_specs=[pl.BlockSpec(memory_space=pltpu.SMEM)] + [pl.BlockSpec(memory_space=pltpu.VMEM)] * 8,
         out_specs=pl.BlockSpec(memory_space=pltpu.VMEM),
         scratch_shapes=[pltpu.VMEM((heads, bq, 128), F32)] * 3 + [pltpu.VMEM((heads, bq, 128), BF16)] * 4 + [pltpu.VMEM((heads, bq, 128), F32)] * 2 + [pltpu.VMEM((bq, 128), F32)],
-        compiler_params=pltpu.CompilerParams(vmem_limit_bytes=56 << 20),
+        compiler_params=pltpu.CompilerParams(vmem_limit_bytes=40 << 20),
         name="attention_backward",
     )(rng, query, key, value, grads, ids, lse, along, stat_rows)
 
-def halo_kernel(count, parts, own_ref, window_ref, send_sem, recv_sem, local_sem):
-    s = lax.axis_index("seq")
-    core = lax.rem(s, 2)
-    sibling = s + 1 - 2 * core
-    rows = own_ref.shape[0] // parts
-    left, right = s >= 2, s < count - 2
-    greet(
-        [(s >= k, {"seq": s - k}) for k in (1, 2)] + [(s < count - k, {"seq": s + k}) for k in (1, 2)]
-    )
-
-    def own(part, kind, slot, target):
-        at = pl.ds(part * rows, rows)
-        return remote(own_ref.at[at], window_ref.at[slot, at], send_sem.at[kind, part], recv_sem.at[slot, part], seq=target)
-
-    def moved(part, kind, held, slot, target):
-        at = pl.ds(part * rows, rows)
-        return remote(window_ref.at[held, at], window_ref.at[slot, at], send_sem.at[kind, part], recv_sem.at[slot, part], seq=target)
-
-    def first_copies(part):
+class Halo:
+    def __init__(self, count, pieces, send_sem, recv_sem):
+        self.count, self.pieces, self.send_sem, self.recv_sem = count, pieces, send_sem, recv_sem
+        s = self.s = lax.axis_index("seq")
+        self.core = lax.rem(s, 2)
+        self.sibling = s + 1 - 2 * self.core
+        self.left, self.right = s >= 2, s < count - 2
+
+    def greet(self):
+        s, count = self.s, self.count
+        greet([(s >= k, {"seq": s - k}) for k in (1, 2)] + [(s < count - k, {"seq": s + k}) for k in (1, 2)])
+
+    def own(self, part, kind, slot, target):
+        source, window = self.pieces[part]
+        return remote(source, window(slot), self.send_sem.at[kind, part], self.recv_sem.at[slot, part], seq=target)
+
+    def moved(self, part, kind, held, slot, target):
+        window = self.pieces[part][1]
+        return remote(window(held), window(slot), self.send_sem.at[kind, part], self.recv_sem.at[slot, part], seq=target)
+
+    def first_copies(self, part):
+        s, core = self.s, self.core
         return (
-            (right, own(part, 0, 1, s + 2)),
-            (left, own(part, 1, 5, s - 2)),
-            (core == 0, own(part, 2, 2, sibling)),
-            (core == 1, own(part, 2, 4, sibling)),
+            (self.right, self.own(part, 0, 1, s + 2)),
+            (self.left, self.own(part, 1, 5, s - 2)),
+            (core == 0, self.own(part, 2, 2, self.sibling)),
+            (core == 1, self.own(part, 2, 4, self.sibling)),
         )
 
-    def from_left(part):
+    def from_left(self, part):
+        s, core, left, right = self.s, self.core, self.left, self.right
         return (
-            (jnp.logical_and(left, jnp.logical_and(core == 1, right)), moved(part, 3, 1, 0, s + 1)),
-            (jnp.logical_and(left, core == 0), moved(part, 4, 1, 0, sibling)),
-            (jnp.logical_and(left, core == 1), moved(part, 4, 1, 2, sibling)),
+            (jnp.logical_and(left, jnp.logical_and(core == 1, right)), self.moved(part, 3, 1, 0, s + 1)),
+            (jnp.logical_and(left, core == 0), self.moved(part, 4, 1, 0, self.sibling)),
+            (jnp.logical_and(left, core == 1), self.moved(part, 4, 1, 2, self.sibling)),
         )
 
-    def from_right(part):
+    def from_right(self, part):
+        s, core, left, right = self.s, self.core, self.left, self.right
         return (
-            (jnp.logical_and(right, jnp.logical_and(core == 0, left)), moved(part, 5, 5, 6, s - 1)),
-            (jnp.logical_and(right, core == 0), moved(part, 6, 5, 4, sibling)),
-            (jnp.logical_and(right, core == 1), moved(part, 6, 5, 6, sibling)),
+            (jnp.logical_and(right, jnp.logical_and(core == 0, left)), self.moved(part, 5, 5, 6, s - 1)),
+            (jnp.logical_and(right, core == 0), self.moved(part, 6, 5, 4, self.sibling)),
+            (jnp.logical_and(right, core == 1), self.moved(part, 6, 5, 6, self.sibling)),
         )
 
-    def each(copies, act):
+    def each(self, copies, act):
         for present, copy in copies:
             pl.when(present)(functools.partial(act, copy))
 
-    start = lambda copy: copy.start()
-    wait_send = lambda copy: copy.wait_send()
-
-    def arrived(slot, part):
-        own(part, 0, slot, s).wait_recv()
-
+    def send(self, part):
+        self.each(self.first_copies(part), lambda copy: copy.start())
+
+    def arrived(self, slot, part):
+        self.own(part, 0, slot, self.s).wait_recv()
+
+    def relay(self, part):
+        pl.when(self.left)(functools.partial(self.arrived, 1, part))
+        self.each(self.from_left(part), lambda copy: copy.start())
+        pl.when(self.right)(functools.partial(self.arrived, 5, part))
+        self.each(self.from_right(part), lambda copy: copy.start())
+
+    def present(self, slot):
+        block = self.s + slot - REACH
+        return jnp.logical_and(block >= 0, block < self.count)
+
+    def receive(self, slot):
+        for part in range(len(self.pieces)):
+            pl.when(self.present(slot))(functools.partial(self.arrived, slot, part))
+
+    def finish(self):
+        for part in range(len(self.pieces)):
+            self.each(self.first_copies(part) + self.from_left(part) + self.from_right(part), lambda copy: copy.wait_send())
+
+
+def project_kernel(count, parts, own_ref, slots_ref, memory_ref, weight_ref, query_bias_ref, value_bias_ref,
+                   q_ref, k_ref, v_ref, source_ref, window_ref, send_sem, recv_sem):
+    block = own_ref.shape[0]
+    rows = block // parts
+    tile = 256
+    tiles = block // tile
+
+    def piece(part):
+        return own_ref.at[pl.ds(part * rows, rows)], lambda slot: window_ref.at[pl.ds(slot * block + part * rows, rows)]
+
+    halo = Halo(count, [piece(part) for part in range(parts)], send_sem, recv_sem)
+    halo.greet()
     for part in range(parts):
-        each(first_copies(part), start)
-    local = pltpu.make_async_copy(own_ref, window_ref.at[REACH], local_sem)
-    local.start()
+        halo.send(part)
+
+    def project(load, start, keep):
+        hot = (lax.broadcasted_iota(jnp.int32, (32, tile), 0) == slots_ref[0:1, pl.ds(start, tile)]).astype(F32).astype(BF16)
+        tn = (((0,), (0,)), ((), ()))
+        chosen = dot(hot, memory_ref[...], tn)
+        inside = wide(dot(hot, jnp.ones((32, 128), BF16), tn), chosen.shape[1])
+        source = jnp.where(inside > 0.5, chosen, load().astype(F32)).astype(BF16)
+        keep(source)
+        out = pl.ds(start, tile)
+        q_ref[out, :] = (dot(source, weight_ref[0]) + query_bias_ref[...]).astype(BF16) * 0.125
+        k_ref[out, :] = dot(source, weight_ref[1]).astype(BF16)
+        v_ref[out, :] = (dot(source, weight_ref[2]) + value_bias_ref[...]).astype(BF16)
+
+    def own_tile(i, carry):
+        at = pl.ds(pl.multiple_of(i * tile, tile), tile)
+
+        def keep(source):
+            source_ref[at, :] = source
+
+        project(lambda: own_ref[at, :], pl.multiple_of(REACH * block + i * tile, tile), keep)
+        return carry
+
+    lax.fori_loop(0, tiles, own_tile, 0)
     for part in range(parts):
-        pl.when(left)(functools.partial(arrived, 1, part))
-        each(from_left(part), start)
-        pl.when(right)(functools.partial(arrived, 5, part))
-        each(from_right(part), start)
-    local.wait()
-    for part in range(parts):
-        for slot in (0, 2, 4, 6):
-            block = s + slot - REACH
-            pl.when(jnp.logical_and(block >= 0, block < count))(functools.partial(arrived, slot, part))
-        each(first_copies(part) + from_left(part) + from_right(part), wait_send)
-
-
-def gather_window(own, count, collective_id, parts=2):
+        halo.relay(part)
+
+    def two_blocks(low, high):
+        def step(i, carry):
+            slot = low + (high - low) * (i // tiles)
+
+            @pl.when(halo.present(slot))
+            def _():
+                start = pl.multiple_of(slot * block + lax.rem(i, tiles) * tile, tile)
+                project(lambda: window_ref[pl.ds(start, tile), :], start, lambda source: None)
+
+            return carry
+
+        lax.fori_loop(0, 2 * tiles, step, 0)
+
+    two_blocks(1, 5)
+    for slots in ((2, 4), (0, 6)):
+        for slot in slots:
+            halo.receive(slot)
+        two_blocks(*slots)
+    halo.finish()
+
+
+def project_window(own, slots, memory, weight, query_bias, value_bias, count, collective_id, parts=2):
+    rows, dim = own.shape
+    width = weight.shape[2]
+    total = (2 * REACH + 1) * rows
+    wide_out = jax.ShapeDtypeStruct((total, width), BF16)
     return pl.pallas_call(
-        functools.partial(halo_kernel, count, parts),
-        out_shape=jax.ShapeDtypeStruct((2 * REACH + 1,) + own.shape, own.dtype),
-        in_specs=[VMEM],
-        out_specs=VMEM,
+        functools.partial(project_kernel, count, parts),
+        out_shape=(wide_out, wide_out, wide_out, jax.ShapeDtypeStruct((rows, dim), BF16)),
+        in_specs=[VMEM] * 6,
+        out_specs=(VMEM,) * 4,
         scratch_shapes=[
+            pltpu.VMEM((total, dim), BF16),
             pltpu.SemaphoreType.DMA((7, parts)),
             pltpu.SemaphoreType.DMA((7, parts)),
-            pltpu.SemaphoreType.DMA,
         ],
-        compiler_params=pltpu.CompilerParams(collective_id=collective_id, has_side_effects=True),
-        name="gather_window",
-    )(own)
+        compiler_params=pltpu.CompilerParams(collective_id=collective_id, has_side_effects=True, vmem_limit_bytes=40 << 20),
+        name="project_window",
+    )(own, slots, memory, weight, query_bias, value_bias)
+
+
+def grads_kernel(count, parts, grad_ref, mixed_ref, lse_ref, window_ref, stats_ref, along_ref, own_stats, send_sem, recv_sem):
+    block, width = grad_ref.shape
+    rows = block // parts
+
+    def piece(part):
+        return grad_ref.at[pl.ds(part * rows, rows)], lambda slot: window_ref.at[pl.ds(slot * block + part * rows, rows)]
+
+    stats_piece = own_stats, lambda slot: stats_ref.at[:, pl.ds(slot * block, block)]
+    halo = Halo(count, [piece(part) for part in range(parts)] + [stats_piece], send_sem, recv_sem)
+    halo.greet()
+    for part in range(parts):
+        halo.send(part)
+    window_ref[REACH * block:(REACH + 1) * block, :] = grad_ref[...]
+    lane = lax.broadcasted_iota(jnp.int32, (block, 128), 1)
+    along = jnp.zeros((block, 128), F32)
+    for pair in range(width // 128):
+        lanes = slice(pair * 128, pair * 128 + 128)
+        product = grad_ref[:, lanes].astype(F32) * mixed_ref[:, lanes].astype(F32)
+        even = jnp.sum(jnp.where(lane < 64, product, 0.0), axis=1, keepdims=True)
+        odd = jnp.sum(jnp.where(lane < 64, 0.0, product), axis=1, keepdims=True)
+        along = jnp.where(lane == 2 * pair, even, jnp.where(lane == 2 * pair + 1, odd, along))
+    along_ref[...] = along
+    own_stats[0:8, :] = jnp.transpose(lse_ref[...])[0:8, :]
+    own_stats[8:16, :] = jnp.transpose(along)[0:8, :]
+    stats_ref[:, REACH * block:(REACH + 1) * block] = own_stats[...]
+    halo.send(parts)
+    for part in range(parts + 1):
+        halo.relay(part)
+    for slot in (0, 2, 4, 6):
+        halo.receive(slot)
+    halo.finish()
+
+
+def gather_grads(grad, mixed, lse, count, collective_id, parts=2):
+    rows, width = grad.shape
+    total = (2 * REACH + 1) * rows
+    return pl.pallas_call(
+        functools.partial(grads_kernel, count, parts),
+        out_shape=(
+            jax.ShapeDtypeStruct((total, width), BF16),
+            jax.ShapeDtypeStruct((16, total), F32),
+            jax.ShapeDtypeStruct((rows, 128), F32),
+        ),
+        in_specs=[VMEM] * 3,
+        out_specs=(VMEM,) * 3,
+        scratch_shapes=[
+            pltpu.VMEM((16, rows), F32),
+            pltpu.SemaphoreType.DMA((7, parts + 1)),
+            pltpu.SemaphoreType.DMA((7, parts + 1)),
+        ],
+        compiler_params=pltpu.CompilerParams(collective_id=collective_id, has_side_effects=True, vmem_limit_bytes=24 << 20),
+        name="gather_grads",
+    )(grad, mixed, lse)
 
 
 def split_dot(left, right, dims):
@@ -286,7 +413,7 @@
 
 
 def tail_kernel(dps, seqs, chunks, chunk, width, up_ref, down_ref, out_grad_ref, proj_ref, source_ref, weight_ref, input1_ref, select_ref, small_ref,
-                up_out, down_out, mix_out, input_out, small_out,
+                up_out, down_out, out_out, qkv_out, input_out, small_out,
                 mix, y_send, y_recv, a_recv, parts, b_recv, mine, c_recv, last, d_recv, small_in, small_recv, small_mine, small_dp,
                 y_sems, a_sems, b_sems, c_sems, d_sems, s_sems):
     zs = seqs // 2
@@ -298,6 +425,7 @@
     owners = small_ref.shape[0]
     block = up_ref.shape[0] // seqs
     rows, columns = proj_ref.shape
+    third = columns // 3
     steps = y_send.shape[0]
     span = rows // steps
     true = s >= 0
@@ -306,7 +434,6 @@
     partners += [(true, {"tensor": 1 - t})]
     greet(partners)
     grads = (up_ref, down_ref, mix)
-    results = (up_out, down_out, mix_out)
     per = up_ref.shape[1] // chunk
 
     def piece(c):
@@ -395,16 +522,25 @@
                     d_copy(c, k).start()
 
     def end_d(c):
-        result = results[c // per]
         at = (c % per) * chunk
 
         def put(share, value):
             for p in range(shares):
                 real = min(width, chunk - p * width)
+                first = at + p * width
 
                 @pl.when(share == p)
                 def _():
-                    result[:, at + p * width:at + p * width + real] = value[:, 0:real].astype(F32)
+                    if c < 2 * per:
+                        (up_out, down_out)[c // per][:, first:first + real] = value[:, 0:real].astype(F32)
+                        return
+                    for lane in range(0, real, 128):
+                        which, column = divmod(first + lane, third)
+                        part = value[:, lane:lane + 128].astype(F32)
+                        if which == 0:
+                            out_out[:, column:column + 128] = part
+                        else:
+                            qkv_out[which - 1, :, column:column + 128] = part
 
         @pl.when(d < shares)
         def _():
@@ -427,11 +563,11 @@
     for c in range(2 * per):
         start_a(c)
     for i in range(steps):
-        y_send[i] = dot(proj_ref[i * span:(i + 1) * span, :], weight_ref[...], NT).astype(BF16)
+        at = slice(i * span, (i + 1) * span)
+        y_send[i] = sum(dot(proj_ref[at, j * third:(j + 1) * third], weight_ref[j], NT) for j in range(3)).astype(BF16)
         y_copy(i).start()
     out_width = out_grad_ref.shape[1]
     mix[:, 0:out_width] = out_grad_ref[...]
-    third = columns // 3
     for i in range(3):
         part = lax.dot_general(source_ref[...], proj_ref[:, i * third:(i + 1) * third], (((0,), (0,)), ((), ())), preferred_element_type=F32)
         mix[:, out_width + i * third:out_width + (i + 1) * third] = part.astype(BF16)
@@ -527,12 +663,13 @@
         out_shape=(
             jax.ShapeDtypeStruct((block, hidden), F32),
             jax.ShapeDtypeStruct((block, hidden), F32),
-            jax.ShapeDtypeStruct((block, hidden), F32),
+            jax.ShapeDtypeStruct((block, out.shape[1]), F32),
+            jax.ShapeDtypeStruct((3, block, out.shape[1]), F32),
             jax.ShapeDtypeStruct((rows, dim), BF16),
             jax.ShapeDtypeStruct(small.shape, F32),
         ),
         in_specs=[VMEM] * 9,
-        out_specs=(VMEM,) * 5,
+        out_specs=(VMEM,) * 6,
         scratch_shapes=[
             pltpu.VMEM((dim, hidden), BF16),
             pltpu.VMEM((steps, rows // steps, dim), BF16),
@@ -615,19 +752,14 @@
     blocks = document_blocks(id_row, own_ids, window_start, bq, bk)
     ids = jnp.broadcast_to(window_ids.astype(F32)[None], (8, pieces * rows))
 
-    tokens_window = gather_window(tokens[0], seqs, 1).reshape(pieces * rows, -1)
-    selector = window_slots[:, None] == jnp.arange(2 * READ_ROWS, dtype=jnp.int32)[None, :]
-    memory_rows = jnp.dot(selector.astype(BF16), memory, preferred_element_type=F32).astype(BF16)
-    source_window = jnp.where((window_slots >= 0)[:, None], memory_rows, tokens_window)
-    projected = jnp.dot(source_window, qkv_weight.reshape(-1, 3 * width), preferred_element_type=F32)
-    query = (projected[:, :width] + query_bias).astype(BF16) * 0.125
-    key = projected[:, width:2 * width].astype(BF16)
-    value = (projected[:, 2 * width:] + value_bias).astype(BF16)
-    here = slice(own, own + rows)
-    source = source_window[here]
-    is_memory = (window_slots[here] >= 0)[:, None]
-
-    mixed_low, logsums = attention_forward(blocks, query[here], key, value, ids, own, bq, bk)
+    weight = qkv_weight.transpose(1, 0, 2)
+    slots_row = jnp.broadcast_to(window_slots[None], (8, pieces * rows))
+    memory_pad = jnp.pad(memory, ((0, 32 - memory.shape[0]), (0, 0)))
+    query, key, value, source = project_window(
+        tokens[0], slots_row, memory_pad, weight, query_bias[None], value_bias[None], seqs, 1)
+    own_slots = window_slots[own:own + rows]
+
+    mixed_low, logsums = attention_forward(blocks, query, key, value, ids, rows, own, bq, bk)
 
     def both(part):
         low = part.astype(BF16)
@@ -654,23 +786,16 @@
     branch_grad = grad_input1.astype(BF16)
     grad_out_weight = jnp.einsum("to,tf->of", branch_grad, mixed_low, preferred_element_type=F32)
     mixed_grad = jnp.einsum("to,of->tf", branch_grad, out_weight, preferred_element_type=F32).astype(BF16)
-    along = jnp.sum((mixed_grad.astype(F32) * mixed_low.astype(F32)).reshape(rows, heads, HEAD_DIM), axis=-1)
-
-    gap = jnp.zeros((rows, 8 - heads), F32)
-    stats = jnp.concatenate([logsums[:, :heads], gap, along, gap], axis=1).T
-    grads_window = gather_window(mixed_grad, seqs, 2).reshape(pieces * rows, -1)
-    stats_window = gather_window(stats, seqs, 3, 1)
-    stats_window = stats_window.transpose(1, 0, 2).reshape(16, pieces * rows)
-    along_cols = jnp.pad(along, ((0, 0), (0, 128 - heads)))
+    grads_window, stats_window, along_cols = gather_grads(mixed_grad, mixed_low, logsums, seqs, 2)
     proj_grad = attention_backward(blocks, query, key, value, grads_window, ids, logsums, along_cols, stats_window, rows, own, bq, bk)
 
-    select = jnp.pad(selector[here].astype(BF16), ((0, 0), (0, 12)))
+    select = (own_slots[:, None] == jnp.arange(32, dtype=jnp.int32)[None, :]).astype(BF16)
     small = jnp.concatenate([
         jnp.stack([grad_gain1, grad_shift1, grad_gain2, grad_shift2, column_sums(branch_grad), column_sums(down_grad)]),
         column_sums(up_grad).reshape(2, -1), jnp.zeros((24, 2 * width), F32)])
-    up_sum, down_sum, mix_sum, input_grad, small = tail(
+    up_sum, down_sum, out_sum, qkv_sum, input_grad, small = tail(
         grad_up_weight.astype(BF16), grad_down_weight.astype(BF16), grad_out_weight.astype(BF16), proj_grad, source,
-        qkv_weight.reshape(-1, 3 * width), grad_input1, select, small.reshape(4, 8, 2 * width), dps, seqs)
+        weight, grad_input1, select, small.reshape(4, 8, 2 * width), dps, seqs)
     small = small.reshape(32, 2 * width)
     input_grad = input_grad[None]
     piece = small.shape[1] // seqs
@@ -678,8 +803,8 @@
     memory_grad = small[9:29]
     return (
         output, input_grad, memory_grad,
-        mix_sum[:, width:].reshape(-1, 3, width), small[8, :width], small[8, width:],
-        mix_sum[:, :width], vectors[4], vectors[0], vectors[1],
+        qkv_sum.transpose(1, 0, 2), small[8, :width], small[8, width:],
+        out_sum, vectors[4], vectors[0], vectors[1],
         up_sum, small[6:8].reshape(-1), down_sum, vectors[5], vectors[2], vectors[3],
     )
 

time: 345 us -> 291 us (0.84)
  other arithmetic: 42.3 us -> 16.6 us
  local copies, waits for them, and re-layouts: 41.6 us -> 24.6 us
  matrix products: 37.5 us -> 23.1 us
  waiting for transfers between devices: 13 us -> 20.1 us
    eq x1 -> x0, other arithmetic: 16.2 us -> none  [on_device(): window_slots[:, None] == jnp.arange(2 * READ_ROWS, dtype=jnp.int32)[None, :]]
    dot_general x2 -> x0, matrix products: 13.4 us -> none  [the longest x1 7.35 us: on_device(): jnp.dot(source_window, qkv_weight.reshape(-1, 3 * width), preferred_eleme...]
    pallas_call x1, Pallas kernels: 21.8 us -> 13.2 us  [attention_backward(): pl.pallas_call(functools.partial(bwd_kernel, bq, bk, own), out_shape=jax....]
    unnamed x84 -> x99, local copies, waits for them, and re-layouts: 18.5 us -> 10.4 us
    pallas_call x3 -> x2, Pallas kernels: 65.6 us -> 73.1 us  [the longest x1 43.8 us: gather_grads(): pl.pallas_call(functools.partial(grads_kernel, count, parts), out_shape=(...]
    ppermute x3, waiting for transfers between devices: 13 us -> 20.1 us  [both(): lax.ppermute(low, 'tensor', [(0, 1), (1, 0)]).astype(F32)]
    slice x1 -> x0, other arithmetic: 6.46 us -> none  [on_device(): key = projected[:, width:2 * width].astype(BF16)]
    reshape x3 -> x0, local copies, waits for them, and re-layouts: 6.3 us -> none  [the longest x1 3.84 us: on_device(): qkv_weight.reshape(-1, 3 * width)]
  transfers between devices with their start and end apart: 3 -> 3, of which waited for: 1 -> 2; matrix products, arithmetic and copies ran while one was open for 10% -> 5% of each run, Pallas kernels for 0% -> 0%
where the time goes in v2:
time: 291 us; the launch traced here: 287 us
  Pallas kernels  194 us (67%)
  local copies, waits for them, and re-layouts  24.6 us (8%)
  matrix products  23.1 us (8%)
  waiting for transfers between devices  20.1 us (7%)
  other arithmetic  16.6 us (6%)
  starting transfers between devices  4.69 us (2%)
  between operations  4.25 us (1%)
    pallas_call x1, Pallas kernels, tail(): pl.pallas_call(functools.partial(tail_kernel, dps, seqs, chunks, chunk, w...  101 us
    pallas_call x1, Pallas kernels, gather_grads(): pl.pallas_call(functools.partial(grads_kernel, count, parts), out_shape=(...  43.8 us
    pallas_call x1, Pallas kernels, project_window(): pl.pallas_call(functools.partial(project_kernel, count, parts), out_shape...  29.3 us
    ppermute x3, waiting for transfers between devices, both(): lax.ppermute(low, 'tensor', [(0, 1), (1, 0)]).astype(F32)  20.1 us
    pallas_call x1, Pallas kernels, attention_backward(): pl.pallas_call(functools.partial(bwd_kernel, bq, bk, own), out_shape=jax....  13.2 us
    unnamed x99, local copies, waits for them, and re-layouts  10.4 us
    dot_general x1, matrix products, on_device(): jnp.dot(first_low, up_weight, preferred_element_type=F32) + up_bias  7.88 us
    pallas_call x1, Pallas kernels, attention_forward(): pl.pallas_call(functools.partial(fwd_kernel, bq, bk, own), out_shape=(jax...  6.34 us
  transfers between devices with their start and end apart: 3, of which 2 were waited for; matrix products, arithmetic and copies ran while one was open for 5% of the time, Pallas kernels for 0%

profile of v2, /device:TPU:0, one launch (start us, length us, event | category | flops | bytes accessed | tf_op | source)
XLA Modules:
  0.0 287.4 jit_solution(5997415697140310379)
XLA Ops:
  0.6 0.0 copy-start
  0.7 1.0 fusion.50
  1.6 0.6 fusion.52
  2.2 3.6 %convert_reduce_fusion.5 = (s32[]{:T(128)}, s32[]{:T(128)}, s32[4096]{0:T(1024)S(1)}) fusion(s32[4096]{0:T(1024)} %bitcast.69, s32[]{:T(128)} %bitcast.3, s32[]{:T(128)} %bitcast.5), kind=kLoop, calls=%fused_computation.103 | loop fusion | flops 282622 | bytes 32784 | tf_op jit(solution)/shard_map/reduce_sum | solution.py:713
  8.5 0.1 fusion.18
  8.6 0.7 broadcast_in_dim.31.query_bias_ref
  9.3 0.7 broadcast_in_dim.32.value_bias_ref
  10.0 0.8 pad.24.memory_ref
  10.7 0.1 pad_add_fusion.rng_ref
  10.8 0.0 copy-start.7
  10.8 1.5 copy-done.7
  12.3 1.1 copy-done.14
  13.4 29.3 %project_window.1 = (bf16[3584,384]{1,0:T(8,128)(2,1)S(1)}, bf16[3584,384]{1,0:T(8,128)(2,1)S(1)}, bf16[3584,384]{1,0:T(8,128)(2,1)S(1)}, bf16[512,768]{1,0:T(8,128)(2,1)S(1)}) custom-call(bf16[512,768]{1,0:T(8,128)(2,1)S(1)} %bitcast.60, s32[8,3584]{1,0:T(8,128)S(1)} %broadcast_in_dim.30.slots_ref, bf16[32,768]{1,0:T(8,128)(2,1)S(1)} %pad.24.memory_ref, ...), custom_call_target="tpu_custom_call" | custom-call | tf_op jit(solution)/shard_map/project_window/pallas_call | solution.py:339
  42.8 6.3 %attention_forward.1 = (bf16[512,384]{1,0:T(8,128)(2,1)S(1)}, f32[512,128]{1,0:T(8,128)S(1)}) custom-call(s32[4]{0:T(128)S(1)} %pad_add_fusion.rng_ref, bf16[3584,384]{1,0:T(8,128)(2,1)S(1)} %get-tuple-element.32.q_ref, bf16[3584,384]{1,0:T(8,128)(2,1)S(1)} %get-tuple-element.33.k_ref, bf16[3584,384]{1,0:T(8,128)(2,1)S(1)} %get-tuple-element.34.v_ref, ...), custom_call_target="tpu_custom_call" | custom-call | tf_op jit(solution)/shard_map/attention_forward/pallas_call | solution.py:123
  49.2 0.6 copy-done.12
  49.9 0.6 convolution_convert_fusion.4
  50.5 1.6 collective-permute-start
  52.0 10.5 %collective-permute-done = bf16[512,768]{1,0:T(8,128)(2,1)S(1)} collective-permute-done((bf16[512,768]{1,0:T(8,128)(2,1)S(1)}, bf16[512,768]{1,0:T(8,128)(2,1)S(1)}, u32[]{:S(2)}, u32[]{:S(2)}) %collective-permute-start) | collective-permute-done | bytes 786464 | tf_op jit(solution)/shard_map/ppermute | solution.py:766
  62.5 0.4 fusion.49
  63.0 0.3 multiply_reduce_fusion.3
  63.4 7.9 %multiply_convert_fusion = (bf16[512,1536]{1,0:T(8,128)(2,1)S(1)}, f32[512,1536]{1,0:T(8,128)S(1)}, f32[512,1536]{1,0:T(8,128)S(1)}) fusion(f32[1536]{0:T(1024)S(1)} %copy-done.45, bf16[768,1536]{1,0:T(8,128)(2,1)S(1)} %copy-done, f32[512,768]{1,0:T(8,128)S(1)} %get-tuple-element.71, f32[768]{0:T(1024)S(1)} %copy-done.42, f32[768]{0:T(1024)S(1)} %copy-done.29, ...), kind=kOutput, calls=%fused_computation.7 | convolution fusion | flops 1261830144 | bytes 11812864 | tf_op jit(solution)/shard_map/dot_general | solution.py:772
  71.3 1.4 convolution_convert_fusion.3
  72.7 1.6 collective-permute-start.1
  74.3 0.8 fusion.14.select_ref
  75.1 9.7 %collective-permute-done.1 = bf16[512,768]{1,0:T(8,128)(2,1)S(1)} collective-permute-done((bf16[512,768]{1,0:T(8,128)(2,1)S(1)}, bf16[512,768]{1,0:T(8,128)(2,1)S(1)}, u32[]{:S(2)}, u32[]{:S(2)}) %collective-permute-start.1) | collective-permute-done | bytes 786464 | tf_op jit(solution)/shard_map/ppermute | solution.py:766
  84.8 0.7 fusion.47
  85.5 0.3 multiply_reduce_fusion.2
  85.9 0.8 copy-done.20
  86.6 1.5 fusion.11
  88.1 1.6 fusion.46
  89.7 1.0 convert_reduce_fusion.2
  90.7 1.4 fusion.53
  92.1 2.0 convert_reduce_fusion
  94.1 2.3 convolution_convert_fusion.2
  96.4 1.5 collective-permute-start.2
  97.9 0.1 convert_reduce_fusion.1
  98.1 0.6 reshape.126
  98.7 1.3 reshape.125
  99.9 1.3 stack.31
  101.2 1.3 reshape.127
  102.5 4.4 %convolution_convert_fusion.down_ref = bf16[768,1536]{1,0:T(8,128)(2,1)} fusion(bf16[512,768]{1,0:T(8,128)(2,1)S(1)} %get-tuple-element.58, bf16[512,1536]{1,0:T(8,128)(2,1)} %copy-done.46), kind=kOutput, calls=%fused_computation.1 | convolution fusion | flops 1209139200 | bytes 4718592 | tf_op jit(solution)/shard_map/to,tf->of/dot_general | solution.py:780
  107.0 3.1 %convolution_convert_fusion.1.up_ref = bf16[768,1536]{1,0:T(8,128)(2,1)} fusion(bf16[512,1536]{1,0:T(8,128)(2,1)S(1)} %copy-done.24, f32[512,768]{1,0:T(8,128)S(1)} %copy-done.16, f32[768]{0:T(1024)S(1)} %copy-done.43, f32[768]{0:T(1024)S(1)} %copy-done.29, f32[512]{0:T(512)S(1)} %fusion.39, f32[512]{0:T(512)S(1)} %broadcast_multiply_fusion.1), kind=kOutput, calls=%fused_computation.2 | convolution fusion | flops 1211105280 | bytes 5515264 | tf_op jit(solution)/shard_map/td,tf->df/dot_general | solution.py:783
  110.1 2.3 multiply_reduce_fusion
  112.5 0.6 fusion.45
  113.2 0.2 convert_reduce_fusion.3
  113.4 1.4 convolution_convert_fusion.5.out_grad_ref
  114.8 0.6 convolution_convert_fusion.6.grad_ref
  115.5 43.8 %gather_grads.1 = (bf16[3584,384]{1,0:T(8,128)(2,1)S(1)}, f32[16,3584]{1,0:T(8,128)S(1)}, f32[512,128]{1,0:T(8,128)S(1)}) custom-call(bf16[512,384]{1,0:T(8,128)(2,1)S(1)} %convolution_convert_fusion.6.grad_ref, bf16[512,384]{1,0:T(8,128)(2,1)S(1)} %get-tuple-element.35.mixed_ref, f32[512,128]{1,0:T(8,128)S(1)} %copy-done.11), custom_call_target="tpu_custom_call" | custom-call | tf_op jit(solution)/shard_map/gather_grads/pallas_call | solution.py:390
  159.3 13.2 %attention_backward.1.proj_ref = bf16[512,1152]{1,0:T(8,128)(2,1)S(1)} custom-call(s32[4]{0:T(128)S(1)} %pad_add_fusion.rng_ref, bf16[3584,384]{1,0:T(8,128)(2,1)S(1)} %copy-done.2, bf16[3584,384]{1,0:T(8,128)(2,1)S(1)} %copy-done.4, bf16[3584,384]{1,0:T(8,128)(2,1)S(1)} %copy-done.6, bf16[3584,384]{1,0:T(8,128)(2,1)S(1)} %get-tuple-element.37.g_ref, ...), custom_call_target="tpu_custom_call" | custom-call | tf_op jit(solution)/shard_map/attention_backward/pallas_call | solution.py:189
  172.6 1.0 copy-done.8
  173.7 1.3 concatenate.38
  174.9 101.3 %tail.1 = (f32[96,1536]{1,0:T(8,128)}, f32[96,1536]{1,0:T(8,128)}, f32[96,384]{1,0:T(8,128)}, f32[3,96,384]{2,1,0:T(8,128)}, bf16[512,768]{1,0:T(8,128)(2,1)}, /*index=5*/f32[4,8,768]{2,1,0:T(8,128)}) custom-call(bf16[768,1536]{1,0:T(8,128)(2,1)} %convolution_convert_fusion.1.up_ref, bf16[768,1536]{1,0:T(8,128)(2,1)} %convolution_convert_fusion.down_ref, ...), custom_call_target="tpu_custom_call" | custom-call | tf_op jit(solution)/shard_map/tail/pallas_call | solution.py:661
  276.3 1.6 slice.162
  277.9 1.3 slice_reduce_fusion
  279.2 0.7 slice.165
  280.0 0.7 slice.166
  280.7 0.1 constant_dynamic-slice_fusion
  280.8 0.5 slice_bitcast_fusion
  281.3 0.6 reshape.130
  281.9 2.1 copy.38
  284.0 0.8 copy.39
  284.8 0.7 copy.40
  285.5 0.8 copy.41
  286.3 0.8 copy.42
  (104 shorter events, 0.3 us)
Async XLA Ops:
  0.6 62.7 %copy-start = (bf16[768,1536]{1,0:T(8,128)(2,1)S(1)}, bf16[768,1536]{1,0:T(8,128)(2,1)}, u32[]{:S(2)}) copy-start(bf16[768,1536]{1,0:T(8,128)(2,1)} %param.27) | copy-start | bytes 7077892
  10.8 1.5 copy-start.7
  12.3 1.1 copy-start.14
  42.8 6.4 %copy-start.1 = (bf16[3584,384]{1,0:T(8,128)(2,1)}, bf16[3584,384]{1,0:T(8,128)(2,1)S(1)}, u32[]{:S(2)}) copy-start(bf16[3584,384]{1,0:T(8,128)(2,1)S(1)} %get-tuple-element.32.q_ref) | copy-start | bytes 8257540
  42.8 6.4 %copy-start.3 = (bf16[3584,384]{1,0:T(8,128)(2,1)}, bf16[3584,384]{1,0:T(8,128)(2,1)S(1)}, u32[]{:S(2)}) copy-start(bf16[3584,384]{1,0:T(8,128)(2,1)S(1)} %get-tuple-element.33.k_ref) | copy-start | bytes 8257540
  42.8 6.4 %copy-start.5 = (bf16[3584,384]{1,0:T(8,128)(2,1)}, bf16[3584,384]{1,0:T(8,128)(2,1)S(1)}, u32[]{:S(2)}) copy-start(bf16[3584,384]{1,0:T(8,128)(2,1)S(1)} %get-tuple-element.34.v_ref) | copy-start | bytes 8257540
  42.8 19.7 %copy-start.9 = (bf16[512,768]{1,0:T(8,128)(2,1)}, bf16[512,768]{1,0:T(8,128)(2,1)S(1)}, u32[]{:S(2)}) copy-start(bf16[512,768]{1,0:T(8,128)(2,1)S(1)} %get-tuple-element.31.source_ref) | copy-start | bytes 2359300
  42.8 7.0 %copy-start.21 = (bf16[768,384]{1,0:T(8,128)(2,1)S(1)}, bf16[768,384]{1,0:T(8,128)(2,1)}, u32[]{:S(2)}) copy-start(bf16[768,384]{1,0:T(8,128)(2,1)} %param.23) | copy-start | bytes 1769476
  49.2 0.6 copy-start.12
  49.8 13.1 %copy-start.10 = (f32[512,128]{1,0:T(8,128)}, f32[512,128]{1,0:T(8,128)S(1)}, u32[]{:S(2)}) copy-start(f32[512,128]{1,0:T(8,128)S(1)} %get-tuple-element.36.lse_ref) | copy-start | bytes 786436
  49.9 12.7 %copy-start.40 = (f32[768]{0:T(1024)S(1)}, f32[768]{0:T(1024)}, u32[]{:S(2)}) copy-start(f32[768]{0:T(1024)} %param.24) | copy-start | bytes 9220
  50.5 12.1 %collective-permute-start = (bf16[512,768]{1,0:T(8,128)(2,1)S(1)}, bf16[512,768]{1,0:T(8,128)(2,1)S(1)}, u32[]{:S(2)}, u32[]{:S(2)}) collective-permute-start(bf16[512,768]{1,0:T(8,128)(2,1)S(1)} %convolution_convert_fusion.4), channel_id=1, source_target_pairs={{0,1},{1,0},{2,3},{3,2},{4,5},{5,4},{6,7},{7,6},{8,9},{9,8},{10,11... | collective-permute-start | bytes 2359304 | tf_op jit(solution)/shard_map/ppermute | solution.py:766
  62.5 0.8 copy-start.29
  62.5 0.8 copy-start.42
  62.5 0.8 copy-start.45
  63.0 21.8 %copy-start.15 = (f32[512,768]{1,0:T(8,128)}, f32[512,768]{1,0:T(8,128)S(1)}, u32[]{:S(2)}) copy-start(f32[512,768]{1,0:T(8,128)S(1)} %get-tuple-element.71) | copy-start | bytes 4718596
  63.3 8.0 %copy-start.31 = (f32[512]{0:T(512)}, f32[512]{0:T(512)S(1)}, u32[]{:S(2)}) copy-start(f32[512]{0:T(512)S(1)} %multiply_reduce_fusion.3) | copy-start | bytes 6148
  63.4 7.9 %copy-start.44 = (bf16[768,1536]{1,0:T(8,128)(2,1)S(1)}, bf16[768,1536]{1,0:T(8,128)(2,1)}, u32[]{:S(2)}) copy-start(bf16[768,1536]{1,0:T(8,128)(2,1)} %param.29) | copy-start | bytes 7077892
  71.3 1.5 copy-start.46
  71.3 13.5 %copy-start.41 = (f32[768]{0:T(1024)S(1)}, f32[768]{0:T(1024)}, u32[]{:S(2)}) copy-start(f32[768]{0:T(1024)} %param.30) | copy-start | bytes 9220
  72.7 12.1 %collective-permute-start.1 = (bf16[512,768]{1,0:T(8,128)(2,1)S(1)}, bf16[512,768]{1,0:T(8,128)(2,1)S(1)}, u32[]{:S(2)}, u32[]{:S(2)}) collective-permute-start(bf16[512,768]{1,0:T(8,128)(2,1)S(1)} %convolution_convert_fusion.3), channel_id=1, source_target_pairs={{0,1},{1,0},{2,3},{3,2},{4,5},{5,4},{6,7},{7,6},{8,9},{9,8},{10,11... | collective-permute-start | bytes 2359304 | tf_op jit(solution)/shard_map/ppermute | solution.py:766
  75.1 10.7 %copy-start.35 = (f32[768]{0:T(1024)S(1)}, f32[768]{0:T(1024)}, u32[]{:S(2)}) copy-start(f32[768]{0:T(1024)} %param.31) | copy-start | bytes 9220
  85.5 1.1 copy-start.20
  85.5 2.6 copy-start.39
  89.7 2.4 copy-start.18
  89.7 2.4 copy-start.33
  94.1 2.3 copy-start.23
  96.4 13.7 %collective-permute-start.2 = (bf16[512,768]{1,0:T(8,128)(2,1)}, bf16[512,768]{1,0:T(8,128)(2,1)}, u32[]{:S(2)}, u32[]{:S(2)}) collective-permute-start(bf16[512,768]{1,0:T(8,128)(2,1)} %convolution_convert_fusion.2), channel_id=1, source_target_pairs={{0,1},{1,0},{2,3},{3,2},{4,5},{5,4},{6,7},{7,6},{8,9},{9,8},{10,11... | collective-permute-start | bytes 2359304 | tf_op jit(solution)/shard_map/ppermute | solution.py:766
  102.5 4.4 %copy-start.16 = (f32[512,768]{1,0:T(8,128)S(1)}, f32[512,768]{1,0:T(8,128)}, u32[]{:S(2)}) copy-start(f32[512,768]{1,0:T(8,128)} %copy-done.15) | copy-start | bytes 4718596
  102.5 4.4 %copy-start.24 = (bf16[512,1536]{1,0:T(8,128)(2,1)S(1)}, bf16[512,1536]{1,0:T(8,128)(2,1)}, u32[]{:S(2)}) copy-start(bf16[512,1536]{1,0:T(8,128)(2,1)} %copy-done.23) | copy-start | bytes 4718596
  102.5 4.4 %copy-start.43 = (f32[768]{0:T(1024)S(1)}, f32[768]{0:T(1024)}, u32[]{:S(2)}) copy-start(f32[768]{0:T(1024)} %param.26) | copy-start | bytes 9220
  107.0 3.1 %copy-start.19 = (f32[512,768]{1,0:T(8,128)S(1)}, f32[512,768]{1,0:T(8,128)}, u32[]{:S(2)}) copy-start(f32[512,768]{1,0:T(8,128)} %copy-done.18) | copy-start | bytes 4718596
  107.0 3.1 %copy-start.34 = (f32[512]{0:T(512)S(1)}, f32[512]{0:T(512)}, u32[]{:S(2)}) copy-start(f32[512]{0:T(512)} %copy-done.33) | copy-start | bytes 6148
  110.1 2.4 copy-start.32
  113.1 1.7 copy-start.22
  113.2 46.1 %copy-start.6 = (bf16[3584,384]{1,0:T(8,128)(2,1)S(1)}, bf16[3584,384]{1,0:T(8,128)(2,1)}, u32[]{:S(2)}) copy-start(bf16[3584,384]{1,0:T(8,128)(2,1)} %copy-done.5) | copy-start | bytes 8257540
  113.4 2.1 copy-start.17
  113.4 2.1 copy-start.11
  113.4 45.9 %copy-start.4 = (bf16[3584,384]{1,0:T(8,128)(2,1)S(1)}, bf16[3584,384]{1,0:T(8,128)(2,1)}, u32[]{:S(2)}) copy-start(bf16[3584,384]{1,0:T(8,128)(2,1)} %copy-done.3) | copy-start | bytes 8257540
  114.8 44.4 %copy-start.2 = (bf16[3584,384]{1,0:T(8,128)(2,1)S(1)}, bf16[3584,384]{1,0:T(8,128)(2,1)}, u32[]{:S(2)}) copy-start(bf16[3584,384]{1,0:T(8,128)(2,1)} %copy-done.1) | copy-start | bytes 8257540
  114.8 44.5 %copy-start.13 = (f32[8,3584]{1,0:T(8,128)S(1)}, f32[8,3584]{1,0:T(8,128)}, u32[]{:S(2)}) copy-start(f32[8,3584]{1,0:T(8,128)} %copy-done.12) | copy-start | bytes 344068
  159.3 14.3 %copy-start.30 = (f32[2,768]{1,0:T(2,128)S(1)}, f32[2,768]{1,0:T(2,128)}, u32[]{:S(2)}) copy-start(f32[2,768]{1,0:T(2,128)} %reshape.127) | copy-start | bytes 18436
  159.3 14.3 %copy-start.36 = (f32[1,768]{1,0:T(1,128)S(1)}, f32[1,768]{1,0:T(1,128)}, u32[]{:S(2)}) copy-start(f32[1,768]{1,0:T(1,128)} %reshape.126) | copy-start | bytes 9220
  159.3 14.3 %copy-start.37 = (f32[1,768]{1,0:T(1,128)S(1)}, f32[1,768]{1,0:T(1,128)}, u32[]{:S(2)}) copy-start(f32[1,768]{1,0:T(1,128)} %reshape.125) | copy-start | bytes 9220
  159.3 14.3 %copy-start.38 = (f32[1,768]{1,0:T(1,128)S(1)}, f32[1,768]{1,0:T(1,128)}, u32[]{:S(2)}) copy-start(f32[1,768]{1,0:T(1,128)} %stack.31) | copy-start | bytes 9220
  172.6 1.0 copy-start.8
  276.3 7.8 %copy-start.27 = (f32[3,96,384]{2,1,0:T(8,128)S(1)}, f32[3,96,384]{2,1,0:T(8,128)}, u32[]{:S(2)}) copy-start(f32[3,96,384]{2,1,0:T(8,128)} %get-tuple-element.42) | copy-start | bytes 1327108
  276.3 8.6 %copy-start.28 = (f32[96,384]{1,0:T(8,128)S(1)}, f32[96,384]{1,0:T(8,128)}, u32[]{:S(2)}) copy-start(f32[96,384]{1,0:T(8,128)} %get-tuple-element.107) | copy-start | bytes 442372
  276.3 9.2 %copy-start.26 = (f32[96,1536]{1,0:T(8,128)S(1)}, f32[96,1536]{1,0:T(8,128)}, u32[]{:S(2)}) copy-start(f32[96,1536]{1,0:T(8,128)} %get-tuple-element.111) | copy-start | bytes 1769476
  281.9 4.4 %copy-start.25 = (f32[96,1536]{1,0:T(8,128)S(1)}, f32[96,1536]{1,0:T(8,128)}, u32[]{:S(2)}) copy-start(f32[96,1536]{1,0:T(8,128)} %get-tuple-element.113) | copy-start | bytes 1769476
